TPU v7x, 256 devices: a whole 4x4x8 slice. The times are simulated.
256 devices in a mesh: date: 32 (over y, x, core), row: 8 (over z).
Axes of the slice: x: 4, y: 4, z: 8, core: 2. Of those that a mesh axis runs over, the one named last changes fastest.
Arguments:
- slc: float32 [2, 32, 64, 4096], P(None, 'date', 'row'), may hold values from -6 to 6
- offsets: int32 [2, 32], replicated, may hold values from -2 to 2, as said below
- masks: int32 [5, 64, 4096], P(None, 'row', 'date'), may hold values from 0 to 262143, as said below
Outputs:
- linked: float32 [2, 32, 64, 4096], P(None, None, 'row', 'date')
- eigen: float32 [64, 4096], P('row', 'date')
Inputs may be any that keep to these rules, and one draw needn't show every extreme that they name: `offsets`: row offset in the first row, column offset in the second; some date has 2 in both and another date -2 in both. `masks`: bit (k mod 18) of word k // 18 tells whether slot k of the pixel's neighbourhood is used; the centre slot 40 is always set; bits of slots 81 and above are zero.
All inputs are finite; a program needn't handle non-finite values.
Results may differ from a plain program's by a relative error of at most 0.00011.
Values sent between devices are 32-bit elements; how exact they have to be, the bound alone decides.
A program may use at most 64 MiB of HBM per device.

v0:
```python
import jax
import jax.numpy as jnp
from jax import lax
from jax.sharding import PartitionSpec as P

NDATE = 32
HALF = 4
SHIFT = 2
ITERS = 2
SLOTS = 81


TAPS = (-0.0625, 0.5625, 0.5625, -0.0625)
EPSILON = 1e-06


def extended(cells, sides, width):
    for axis, dim in sides:
        count = lax.axis_size(axis)
        ends = count - 1
        head = lax.slice_in_dim(cells, 0, width, axis=dim)
        tail = lax.slice_in_dim(cells, cells.shape[dim] - width, cells.shape[dim], axis=dim)
        cells = jnp.concatenate(
            [
                lax.ppermute(tail, axis, [(i, (i + 1) % count) for i in range(ends)]),
                cells,
                lax.ppermute(head, axis, [((i + 1) % count, i) for i in range(ends)]),
            ],
            axis=dim,
        )
    return cells


def shift_mix(image_plane, shifts, margin, out_rows, out_cols):
    row_taps = lax.dynamic_slice_in_dim(image_plane, margin - 1 + shifts[0], out_rows + 3, 1)
    row_mixed = TAPS[0] * row_taps[:, 0:out_rows]
    for tap_index in range(1, 4):
        row_mixed = row_mixed + TAPS[tap_index] * row_taps[:, tap_index : tap_index + out_rows]
    col_taps = lax.dynamic_slice_in_dim(row_mixed, margin - 1 + shifts[1], out_cols + 3, 2)
    col_mixed = TAPS[0] * col_taps[:, :, 0:out_cols]
    for tap_index in range(1, 4):
        col_mixed = col_mixed + TAPS[tap_index] * col_taps[:, :, tap_index : tap_index + out_cols]
    return col_mixed


def unpack_bits(mask_words):
    shift_ids = jnp.arange(18, dtype=jnp.int32)
    spread = jnp.right_shift(mask_words[:, None, :], shift_ids[None, :, None]) & 1
    return spread.reshape(-1, mask_words.shape[-1])[:SLOTS].astype(jnp.float32)


def power_norm(vec_real, vec_imag):
    return jnp.sqrt(jnp.sum(vec_real * vec_real + vec_imag * vec_imag, axis=0) + EPSILON)


def link_phases(patches, mask_bits):
    dates = patches.shape[0] // 2
    population = jnp.sum(mask_bits, axis=0)
    weighted = patches * mask_bits[None]
    gram_matrix = (
        jnp.einsum("ikp,jkp->ijp", weighted, patches, precision=lax.Precision.HIGHEST) / population
    )
    cov_real = gram_matrix[:dates, :dates] + gram_matrix[dates:, dates:]
    cov_imag = gram_matrix[dates:, :dates] - gram_matrix[:dates, dates:]
    vec_real = jnp.ones((dates, patches.shape[-1]), jnp.float32)
    vec_imag = jnp.zeros((dates, patches.shape[-1]), jnp.float32)
    norm_prev = power_norm(vec_real, vec_imag)
    for step_index in range(ITERS):
        norm_prev = power_norm(vec_real, vec_imag)
        next_real = jnp.einsum(
            "tup,up->tp", cov_real, vec_real, precision=lax.Precision.HIGHEST
        ) - jnp.einsum("tup,up->tp", cov_imag, vec_imag, precision=lax.Precision.HIGHEST)
        next_imag = jnp.einsum(
            "tup,up->tp", cov_real, vec_imag, precision=lax.Precision.HIGHEST
        ) + jnp.einsum("tup,up->tp", cov_imag, vec_real, precision=lax.Precision.HIGHEST)
        vec_real, vec_imag = (next_real, next_imag)
    norm_last = power_norm(vec_real, vec_imag)
    linked = jnp.stack([vec_real, vec_imag]) * (jnp.sqrt(jnp.float32(dates)) / norm_last)
    return (linked, norm_last / norm_prev)


def on_device(slc, offsets, masks):
    dates_dev = slc.shape[1]
    rows_dev = slc.shape[2]
    cols_all = slc.shape[3]
    margin = SHIFT + 2
    side = 2 * HALF + 1
    own_shifts = lax.dynamic_slice_in_dim(offsets, lax.axis_index("date") * dates_dev, dates_dev, 1)
    rimmed = extended(slc, (("row", 2),), margin)
    rimmed = jnp.pad(rimmed, ((0, 0), (0, 0), (0, 0), (margin, margin)))
    outgoing = jax.vmap(
        lambda image_plane, shifts: shift_mix(image_plane, shifts, margin, rows_dev, cols_all),
        in_axes=(1, 1),
        out_axes=1,
    )(rimmed, own_shifts)
    regrouped = lax.all_to_all(outgoing, "date", split_axis=3, concat_axis=1, tiled=True)
    cols_dev = regrouped.shape[3]
    window = extended(regrouped, (("row", 2), ("date", 3)), HALF)

    def one_row(row_index):
        row_block = lax.dynamic_slice_in_dim(window, row_index, side, 2)
        patches = jnp.stack(
            [row_block[..., col_step : col_step + cols_dev] for col_step in range(side)], axis=3
        )
        patches = patches.reshape(2 * NDATE, SLOTS, cols_dev)
        mask_bits = unpack_bits(lax.dynamic_index_in_dim(masks, row_index, 1, keepdims=False))
        return link_phases(patches, mask_bits)

    linked_rows, eigen_rows = lax.map(one_row, jnp.arange(rows_dev, dtype=jnp.int32))
    return (jnp.transpose(linked_rows, (1, 2, 0, 3)), eigen_rows)


def solution(mesh):
    in_specs = (P(None, "date", "row", None), P(), P(None, "row", "date"))
    out_specs = (P(None, None, "row", "date"), P("row", "date"))
    return jax.shard_map(
        on_device, mesh=mesh, in_specs=in_specs, out_specs=out_specs, check_vma=False
    )
```

profile of v0, /device:TPU:39, one launch (start us, length us, event | category | flops | bytes accessed | tf_op | source)
XLA Modules:
  0.0 382.7 jit_solution(16343542227004659011)
XLA Ops:
  13.8 4.4 %copy.76 = f32[2,1,8,4096]{2,0,1,3:T(2,128)} copy(f32[2,1,8,4096]{3,2,0,1:T(8,128)S(1)} %fusion.22) | data formatting | bytes 524288 | tf_op jit(solution)/shard_map/vmap()/transpose | solution.py:91
  18.2 7.2 %reshape.162 = f32[32,1,2048]{2,1,0:T(1,128)S(1)} reshape(f32[4096,1,2,8]{3,2,1,0:T(2,128)} %bitcast.181) | data formatting | bytes 524288
  25.4 16.1 %all_to_all.18 = f32[32,1,2048]{2,1,0:T(1,128)S(1)} all-to-all(f32[32,1,2048]{2,1,0:T(1,128)S(1)} %reshape.162), channel_id=1, replica_groups=mesh['date'=32,'row'=8] {'date'}, dimensions={0} | all-to-all | bytes 524288 | tf_op jit(solution)/shard_map/all_to_all | solution.py:96
  43.3 7.6 %reshape.163 = f32[4096,1,2,8]{3,2,1,0:T(2,128)} reshape(f32[32,2048]{1,0:T(8,128)S(1)} %reduce.16) | data formatting | bytes 524288
  50.9 5.1 %copy.77 = f32[2,1,8,4096]{3,1,2,0:T(1,128)S(1)} copy(f32[2,1,8,4096]{2,0,1,3:T(2,128)} %bitcast.182) | data formatting | bytes 524288 | tf_op jit(solution)/shard_map/all_to_all | solution.py:96
  56.1 4.8 %collective-permute-start.2 = (f32[2,32,4,128]{3,1,2,0:T(8,128)S(1)}, f32[2,32,4,128]{3,1,2,0:T(8,128)S(1)}, u32[]{:S(2)}, u32[]{:S(2)}) collective-permute-start(f32[2,32,4,128]{3,1,2,0:T(8,128)S(1)} %get-tuple-element.146), channel_id=1, source_target_pairs={{0,1},{1,2},{2,3},{3,4},{4,5},{5,6},{6,7},{8,9},{9,10},{10,11},{11... | collective-permute-start | bytes 393224 | tf_op jit(solution)/shard_map/ppermute | solution.py:25
  63.8 5.3 %collective-permute-done.3 = f32[2,32,4,128]{3,1,2,0:T(8,128)S(1)} collective-permute-done((f32[2,32,4,128]{3,1,2,0:T(8,128)S(1)}, f32[2,32,4,128]{3,1,2,0:T(8,128)S(1)}, u32[]{:S(2)}, u32[]{:S(2)}) %collective-permute-start.3) | collective-permute-done | bytes 131104 | tf_op jit(solution)/shard_map/ppermute | solution.py:27
  69.4 4.1 %collective-permute-start.4 = (f32[2,32,16,4]{3,1,2,0:T(8,128)S(1)}, f32[2,32,16,4]{3,1,2,0:T(8,128)S(1)}, u32[]{:S(2)}, u32[]{:S(2)}) collective-permute-start(f32[2,32,16,4]{3,1,2,0:T(8,128)S(1)} %get-tuple-element.140), channel_id=1, source_target_pairs={{0,8},{8,16},{16,24},{24,32},{32,40},{40,48},{48,56},{56,64},{64,7... | collective-permute-start | bytes 49160 | tf_op jit(solution)/shard_map/ppermute | solution.py:25
  75.6 4.0 %collective-permute-done.4 = f32[2,32,16,4]{3,1,2,0:T(8,128)S(1)} collective-permute-done((f32[2,32,16,4]{3,1,2,0:T(8,128)S(1)}, f32[2,32,16,4]{3,1,2,0:T(8,128)S(1)}, u32[]{:S(2)}, u32[]{:S(2)}) %collective-permute-start.4) | collective-permute-done | bytes 16416 | tf_op jit(solution)/shard_map/ppermute | solution.py:25
  79.6 6.5 %collective-permute-done.5 = f32[2,32,16,4]{3,1,2,0:T(8,128)S(1)} collective-permute-done((f32[2,32,16,4]{3,1,2,0:T(8,128)S(1)}, f32[2,32,16,4]{3,1,2,0:T(8,128)S(1)}, u32[]{:S(2)}, u32[]{:S(2)}) %collective-permute-start.5) | collective-permute-done | bytes 16416 | tf_op jit(solution)/shard_map/ppermute | solution.py:27
  87.6 294.3 %while.14 = (s32[]{:T(128)}, f32[8,2,32,128]{3,0,2,1:T(8,128)S(1)}, f32[8,128]{1,0:T(8,128)S(1)}, s32[8]{0:T(128)S(1)}, f32[2,32,16,136]{3,1,2,0:T(8,128)}, /*in...) while((s32[]{:T(128)}, f32[8,2,32,128]{3,0,2,1:T(8,128)S(1)}, ...), condition=%wide.region_4.5_spmd, body=%wide.region_0.4_spmd.sunk | while | flops 512975488 | bytes 39309560 | solution.py:109
  90.2 4.3 %constant_dynamic-slice_fusion.14 = (f32[2,32,9,128]{3,1,2,0:T(8,128)S(1)}, f32[2,32,9,128]{3,1,2,0:T(8,128)S(1)}, f32[2,32,9,128]{3,1,2,0:T(8,128)S(1)}, f32[2,...) fusion(f32[2,32,16,136]{3,1,2,0:T(8,128)} %get-tuple-element.28, ...), kind=kLoop, calls=%fused_computation.54.clone.1 | loop fusion | bytes 5308452 | tf_op jit(solution)/shard_map/while/body/eval_jaxpr/slice | solution.py:103
  98.9 4.9 %copy.212 = f32[64,81,128]{1,0,2:T(8,128)} copy(f32[64,81,128]{2,0,1:T(8,128)} %broadcast_multiply_fusion.2) | data formatting | bytes 5308416 | tf_op jit(solution)/shard_map/while/body/eval_jaxpr/mul | solution.py:59
  107.3 9.2 %divide_bitcast_fusion.2 = f32[64,64,128]{0,1,2:T(8,128)S(1)} fusion(f32[128]{0:T(128)S(1)} %get-tuple-element.217, f32[64,81,128]{1,0,2:T(8,128)} %copy.211, f32[64,81,128]{1,0,2:T(8,128)} %copy.212), kind=kOutput, calls=%fused_computation.clone.1 | convolution fusion | flops 510132224 | bytes 7406080 | tf_op jit(solution)/shard_map/while/body/eval_jaxpr/ikp,jkp->ijp/dot_general | solution.py:61
  127.2 4.2 %constant_dynamic-slice_fusion.14 = (f32[2,32,9,128]{3,1,2,0:T(8,128)S(1)}, f32[2,32,9,128]{3,1,2,0:T(8,128)S(1)}, f32[2,32,9,128]{3,1,2,0:T(8,128)S(1)}, f32[2,...) fusion(f32[2,32,16,136]{3,1,2,0:T(8,128)} %get-tuple-element.28, ...), kind=kLoop, calls=%fused_computation.54.clone.1 | loop fusion | bytes 5308452 | tf_op jit(solution)/shard_map/while/body/eval_jaxpr/slice | solution.py:103
  135.9 4.9 %copy.212 = f32[64,81,128]{1,0,2:T(8,128)} copy(f32[64,81,128]{2,0,1:T(8,128)} %broadcast_multiply_fusion.2) | data formatting | bytes 5308416 | tf_op jit(solution)/shard_map/while/body/eval_jaxpr/mul | solution.py:59
  144.3 9.2 %divide_bitcast_fusion.2 = f32[64,64,128]{0,1,2:T(8,128)S(1)} fusion(f32[128]{0:T(128)S(1)} %get-tuple-element.217, f32[64,81,128]{1,0,2:T(8,128)} %copy.211, f32[64,81,128]{1,0,2:T(8,128)} %copy.212), kind=kOutput, calls=%fused_computation.clone.1 | convolution fusion | flops 510132224 | bytes 7406080 | tf_op jit(solution)/shard_map/while/body/eval_jaxpr/ikp,jkp->ijp/dot_general | solution.py:61
  164.2 4.1 %constant_dynamic-slice_fusion.14 = (f32[2,32,9,128]{3,1,2,0:T(8,128)S(1)}, f32[2,32,9,128]{3,1,2,0:T(8,128)S(1)}, f32[2,32,9,128]{3,1,2,0:T(8,128)S(1)}, f32[2,...) fusion(f32[2,32,16,136]{3,1,2,0:T(8,128)} %get-tuple-element.28, ...), kind=kLoop, calls=%fused_computation.54.clone.1 | loop fusion | bytes 5308452 | tf_op jit(solution)/shard_map/while/body/eval_jaxpr/slice | solution.py:103
  172.8 4.9 %copy.212 = f32[64,81,128]{1,0,2:T(8,128)} copy(f32[64,81,128]{2,0,1:T(8,128)} %broadcast_multiply_fusion.2) | data formatting | bytes 5308416 | tf_op jit(solution)/shard_map/while/body/eval_jaxpr/mul | solution.py:59
  181.2 9.2 %divide_bitcast_fusion.2 = f32[64,64,128]{0,1,2:T(8,128)S(1)} fusion(f32[128]{0:T(128)S(1)} %get-tuple-element.217, f32[64,81,128]{1,0,2:T(8,128)} %copy.211, f32[64,81,128]{1,0,2:T(8,128)} %copy.212), kind=kOutput, calls=%fused_computation.clone.1 | convolution fusion | flops 510132224 | bytes 7406080 | tf_op jit(solution)/shard_map/while/body/eval_jaxpr/ikp,jkp->ijp/dot_general | solution.py:61
  201.1 4.1 %constant_dynamic-slice_fusion.14 = (f32[2,32,9,128]{3,1,2,0:T(8,128)S(1)}, f32[2,32,9,128]{3,1,2,0:T(8,128)S(1)}, f32[2,32,9,128]{3,1,2,0:T(8,128)S(1)}, f32[2,...) fusion(f32[2,32,16,136]{3,1,2,0:T(8,128)} %get-tuple-element.28, ...), kind=kLoop, calls=%fused_computation.54.clone.1 | loop fusion | bytes 5308452 | tf_op jit(solution)/shard_map/while/body/eval_jaxpr/slice | solution.py:103
  209.6 4.9 %copy.212 = f32[64,81,128]{1,0,2:T(8,128)} copy(f32[64,81,128]{2,0,1:T(8,128)} %broadcast_multiply_fusion.2) | data formatting | bytes 5308416 | tf_op jit(solution)/shard_map/while/body/eval_jaxpr/mul | solution.py:59
  218.0 9.2 %divide_bitcast_fusion.2 = f32[64,64,128]{0,1,2:T(8,128)S(1)} fusion(f32[128]{0:T(128)S(1)} %get-tuple-element.217, f32[64,81,128]{1,0,2:T(8,128)} %copy.211, f32[64,81,128]{1,0,2:T(8,128)} %copy.212), kind=kOutput, calls=%fused_computation.clone.1 | convolution fusion | flops 510132224 | bytes 7406080 | tf_op jit(solution)/shard_map/while/body/eval_jaxpr/ikp,jkp->ijp/dot_general | solution.py:61
  246.1 4.9 %copy.212 = f32[64,81,128]{1,0,2:T(8,128)} copy(f32[64,81,128]{2,0,1:T(8,128)} %broadcast_multiply_fusion.2) | data formatting | bytes 5308416 | tf_op jit(solution)/shard_map/while/body/eval_jaxpr/mul | solution.py:59
  254.6 9.2 %divide_bitcast_fusion.2 = f32[64,64,128]{0,1,2:T(8,128)S(1)} fusion(f32[128]{0:T(128)S(1)} %get-tuple-element.217, f32[64,81,128]{1,0,2:T(8,128)} %copy.211, f32[64,81,128]{1,0,2:T(8,128)} %copy.212), kind=kOutput, calls=%fused_computation.clone.1 | convolution fusion | flops 510132224 | bytes 7406080 | tf_op jit(solution)/shard_map/while/body/eval_jaxpr/ikp,jkp->ijp/dot_general | solution.py:61
  282.7 4.9 %copy.212 = f32[64,81,128]{1,0,2:T(8,128)} copy(f32[64,81,128]{2,0,1:T(8,128)} %broadcast_multiply_fusion.2) | data formatting | bytes 5308416 | tf_op jit(solution)/shard_map/while/body/eval_jaxpr/mul | solution.py:59
  291.1 9.2 %divide_bitcast_fusion.2 = f32[64,64,128]{0,1,2:T(8,128)S(1)} fusion(f32[128]{0:T(128)S(1)} %get-tuple-element.217, f32[64,81,128]{1,0,2:T(8,128)} %copy.211, f32[64,81,128]{1,0,2:T(8,128)} %copy.212), kind=kOutput, calls=%fused_computation.clone.1 | convolution fusion | flops 510132224 | bytes 7406080 | tf_op jit(solution)/shard_map/while/body/eval_jaxpr/ikp,jkp->ijp/dot_general | solution.py:61
  319.4 4.9 %copy.212 = f32[64,81,128]{1,0,2:T(8,128)} copy(f32[64,81,128]{2,0,1:T(8,128)} %broadcast_multiply_fusion.2) | data formatting | bytes 5308416 | tf_op jit(solution)/shard_map/while/body/eval_jaxpr/mul | solution.py:59
  327.8 9.2 %divide_bitcast_fusion.2 = f32[64,64,128]{0,1,2:T(8,128)S(1)} fusion(f32[128]{0:T(128)S(1)} %get-tuple-element.217, f32[64,81,128]{1,0,2:T(8,128)} %copy.211, f32[64,81,128]{1,0,2:T(8,128)} %copy.212), kind=kOutput, calls=%fused_computation.clone.1 | convolution fusion | flops 510132224 | bytes 7406080 | tf_op jit(solution)/shard_map/while/body/eval_jaxpr/ikp,jkp->ijp/dot_general | solution.py:61
  347.7 4.0 %constant_dynamic-slice_fusion.14 = (f32[2,32,9,128]{3,1,2,0:T(8,128)S(1)}, f32[2,32,9,128]{3,1,2,0:T(8,128)S(1)}, f32[2,32,9,128]{3,1,2,0:T(8,128)S(1)}, f32[2,...) fusion(f32[2,32,16,136]{3,1,2,0:T(8,128)} %get-tuple-element.28, ...), kind=kLoop, calls=%fused_computation.54.clone.1 | loop fusion | bytes 5308452 | tf_op jit(solution)/shard_map/while/body/eval_jaxpr/slice | solution.py:103
  356.2 4.9 %copy.212 = f32[64,81,128]{1,0,2:T(8,128)} copy(f32[64,81,128]{2,0,1:T(8,128)} %broadcast_multiply_fusion.2) | data formatting | bytes 5308416 | tf_op jit(solution)/shard_map/while/body/eval_jaxpr/mul | solution.py:59
  364.6 9.2 %divide_bitcast_fusion.2 = f32[64,64,128]{0,1,2:T(8,128)S(1)} fusion(f32[128]{0:T(128)S(1)} %get-tuple-element.217, f32[64,81,128]{1,0,2:T(8,128)} %copy.211, f32[64,81,128]{1,0,2:T(8,128)} %copy.212), kind=kOutput, calls=%fused_computation.clone.1 | convolution fusion | flops 510132224 | bytes 7406080 | tf_op jit(solution)/shard_map/while/body/eval_jaxpr/ikp,jkp->ijp/dot_general | solution.py:61
  (336 shorter events, 153.5 us)
Async XLA Ops:
  0.6 6.6 %copy-start = (s32[2,32]{1,0:T(2,128)S(1)}, s32[2,32]{1,0:T(2,128)}, u32[]{:S(2)}) copy-start(s32[2,32]{1,0:T(2,128)} %param.6) | copy-start | bytes 772
  1.8 8.7 %collective-permute-start = (f32[2,1,4,4096]{3,2,1,0:T(4,128)S(1)}, f32[2,1,4,4096]{3,2,1,0:T(4,128)S(1)}, u32[]{:S(2)}, u32[]{:S(2)}) collective-permute-start(f32[2,1,4,4096]{3,2,1,0:T(4,128)S(1)} %get-tuple-element.148), channel_id=1, source_target_pairs={{0,1},{1,2},{2,3},{3,4},{4,5},{5,6},{6,7},{8,9},{9,10},{10,11},{11... | collective-permute-start | bytes 393224 | tf_op jit(solution)/shard_map/ppermute | solution.py:25
  5.3 6.3 %collective-permute-start.1 = (f32[2,1,4,4096]{3,2,1,0:T(4,128)S(1)}, f32[2,1,4,4096]{3,2,1,0:T(4,128)S(1)}, u32[]{:S(2)}, u32[]{:S(2)}) collective-permute-start(f32[2,1,4,4096]{3,2,1,0:T(4,128)S(1)} %get-tuple-element.149), channel_id=1, source_target_pairs={{1,0},{2,1},{3,2},{4,3},{5,4},{6,5},{7,6},{9,8},{10,9},{11,10},{12... | collective-permute-start | bytes 393224 | tf_op jit(solution)/shard_map/ppermute | solution.py:27
  56.1 7.8 %collective-permute-start.2 = (f32[2,32,4,128]{3,1,2,0:T(8,128)S(1)}, f32[2,32,4,128]{3,1,2,0:T(8,128)S(1)}, u32[]{:S(2)}, u32[]{:S(2)}) collective-permute-start(f32[2,32,4,128]{3,1,2,0:T(8,128)S(1)} %get-tuple-element.146), channel_id=1, source_target_pairs={{0,1},{1,2},{2,3},{3,4},{4,5},{5,6},{6,7},{8,9},{9,10},{10,11},{11... | collective-permute-start | bytes 393224 | tf_op jit(solution)/shard_map/ppermute | solution.py:25
  60.8 8.3 %collective-permute-start.3 = (f32[2,32,4,128]{3,1,2,0:T(8,128)S(1)}, f32[2,32,4,128]{3,1,2,0:T(8,128)S(1)}, u32[]{:S(2)}, u32[]{:S(2)}) collective-permute-start(f32[2,32,4,128]{3,1,2,0:T(8,128)S(1)} %get-tuple-element.147), channel_id=1, source_target_pairs={{1,0},{2,1},{3,2},{4,3},{5,4},{6,5},{7,6},{9,8},{10,9},{11,10},{12... | collective-permute-start | bytes 393224 | tf_op jit(solution)/shard_map/ppermute | solution.py:27
  69.4 10.2 %collective-permute-start.4 = (f32[2,32,16,4]{3,1,2,0:T(8,128)S(1)}, f32[2,32,16,4]{3,1,2,0:T(8,128)S(1)}, u32[]{:S(2)}, u32[]{:S(2)}) collective-permute-start(f32[2,32,16,4]{3,1,2,0:T(8,128)S(1)} %get-tuple-element.140), channel_id=1, source_target_pairs={{0,8},{8,16},{16,24},{24,32},{32,40},{40,48},{48,56},{56,64},{64,7... | collective-permute-start | bytes 49160 | tf_op jit(solution)/shard_map/ppermute | solution.py:25
  73.5 12.6 %collective-permute-start.5 = (f32[2,32,16,4]{3,1,2,0:T(8,128)S(1)}, f32[2,32,16,4]{3,1,2,0:T(8,128)S(1)}, u32[]{:S(2)}, u32[]{:S(2)}) collective-permute-start(f32[2,32,16,4]{3,1,2,0:T(8,128)S(1)} %get-tuple-element.141), channel_id=1, source_target_pairs={{8,0},{16,8},{24,16},{32,24},{40,32},{48,40},{56,48},{64,56},{72,6... | collective-permute-start | bytes 49160 | tf_op jit(solution)/shard_map/ppermute | solution.py:27
  382.0 0.7 copy-start.1
  382.0 0.7 copy-start.2
where the time goes:
time: 385 us; the launch traced here: 383 us
  local copies, waits for them, and re-layouts  148 us (38%)
  other arithmetic  78.1 us (20%)
  matrix products  73.9 us (19%)
  loops' own time  27.1 us (7%)
  starting transfers between devices  18.3 us (5%)
  waiting for transfers between devices  18.1 us (5%)
  blocking collectives  16.1 us (4%)
    dot_general x8, matrix products, link_phases(): jnp.einsum('ikp,jkp->ijp', weighted, patches, precision=lax.Precision.HIG...  73.9 us
    while x16, other arithmetic  56.2 us
    mul x8, local copies, waits for them, and re-layouts, link_phases(): weighted = patches * mask_bits[None]  39 us
    slice x8, local copies, waits for them, and re-layouts, one_row(): row_block[..., col_step:col_step + cols_dev]  32.2 us
    reshape x8, local copies, waits for them, and re-layouts, one_row(): patches = patches.reshape(2 * NDATE, SLOTS, cols_dev)  28.2 us
    another operation x1, loops' own time, on_device(): lax.map(one_row, jnp.arange(rows_dev, dtype=jnp.int32))  27.1 us
    all_to_all x1, blocking collectives, on_device(): lax.all_to_all(outgoing, 'date', split_axis=3, concat_axis=1, tiled=True)  16.1 us
    unnamed x8, local copies, waits for them, and re-layouts  15.6 us
  transfers between devices with their start and end apart: 6, of which 5 were waited for; matrix products, arithmetic and copies ran while one was open for 0% of the time, Pallas kernels for 0%

commit v1 on v0

v1 whole, which is shorter than its diff:
```python
import functools

import jax
import jax.numpy as jnp
from jax import lax
from jax.experimental import pallas as pl
from jax.experimental.pallas import tpu as pltpu
from jax.sharding import PartitionSpec as P

NDATE = 32
COLS = 128
ROWS = 8
PLANES = 2 * NDATE
EPSILON = 1e-06
MESH = pl.DeviceIdType.MESH
F32 = jnp.float32
BF16 = jnp.bfloat16


def iota(shape, axis):
    return lax.broadcasted_iota(jnp.int32, shape, axis)


def pack_rim(slc_ref, rim_ref):
    lane = iota((ROWS, COLS), 1)
    row = iota((ROWS, COLS), 0)
    for dest in range(NDATE):
        for part in range(2):
            if dest > 0:
                left = slc_ref[part, :, (dest - 1) * COLS : dest * COLS]
            else:
                left = jnp.zeros((ROWS, COLS), F32)
            if dest < NDATE - 1:
                right = slc_ref[part, :, (dest + 1) * COLS : (dest + 2) * COLS]
            else:
                right = jnp.zeros((ROWS, COLS), F32)
            both = jnp.where(lane < 8, right, left)
            spread = pltpu.roll(both, 8, 1, stride=16, stride_axis=0)
            spread = jnp.where(lane // 16 == row, spread, 0.0)
            rim_ref[dest, part : part + 1, :] = jnp.sum(spread, axis=0, keepdims=True)


def pack_kernel(slc_ref, rim_ref):
    pack_rim(slc_ref, rim_ref)


def exchange_kernel(
    slc_ref, rim_in, main_ref, rim_ref, own_sem, send_sem, recv_sem, fwd_send, fwd_recv
):
    me = lax.axis_index("date")
    z = lax.axis_index("row")
    last_z = lax.axis_size("row") - 1
    block, place = me // 8, me % 8

    barrier = pltpu.get_barrier_semaphore()
    for s in range(1, NDATE):
        pl.semaphore_signal(
            barrier, inc=1, device_id={"date": (me + s) % NDATE}, device_id_type=MESH
        )

    for s in (1, last_z):
        pl.semaphore_signal(
            barrier, inc=1, device_id={"row": (z + s) % (last_z + 1)}, device_id_type=MESH
        )
    pl.semaphore_wait(barrier, NDATE + 1)

    own = [
        pltpu.make_async_copy(
            slc_ref.at[:, :, pl.ds(pl.multiple_of(me * COLS, COLS), COLS)],
            main_ref.at[1, me],
            own_sem.at[0],
        ),
        pltpu.make_async_copy(rim_in.at[me], rim_ref.at[1, me], own_sem.at[1]),
    ]
    for copy in own:
        copy.start()

    sends = []
    for g in range(4):
        for j in range(8):
            if g == 0 and j == 0:
                continue
            dest = ((block + g) % 4) * 8 + (place + j) % 8
            for which, src, dst in (
                (
                    0,
                    slc_ref.at[:, :, pl.ds(pl.multiple_of(dest * COLS, COLS), COLS)],
                    main_ref.at[1, me],
                ),
                (1, rim_in.at[dest], rim_ref.at[1, me]),
            ):
                copy = pltpu.make_async_remote_copy(
                    src_ref=src,
                    dst_ref=dst,
                    send_sem=send_sem.at[which, g, j],
                    recv_sem=recv_sem.at[which, g, j],
                    device_id={"date": dest},
                    device_id_type=MESH,
                )
                copy.start()
                sends.append((g, j, copy))

    for copy in own:
        copy.wait()

    def forwards(g, side):
        group = (block + 4 - g) % 4
        slot, to = (2, z - 1) if side == 0 else (0, z + 1)
        first = pl.multiple_of(group * 8, 8)
        return [
            pltpu.make_async_remote_copy(
                src_ref=ref.at[1, pl.ds(first, 8)],
                dst_ref=ref.at[slot, pl.ds(first, 8)],
                send_sem=fwd_send.at[which, side, g],
                recv_sem=fwd_recv.at[which, side, g],
                device_id={"row": to},
                device_id_type=MESH,
            )
            for which, ref in ((0, main_ref), (1, rim_ref))
        ]

    for g in range(4):
        for step, _, copy in sends:
            if step == g:
                copy.wait_recv()

        @pl.when(z > 0)
        def _(g=g):
            for copy in forwards(g, 0):
                copy.start()

        @pl.when(z < last_z)
        def _(g=g):
            for copy in forwards(g, 1):
                copy.start()

    for _, _, copy in sends:
        copy.wait_send()
    for g in range(4):

        @pl.when(z > 0)
        def _(g=g):
            for copy in forwards(g, 0):
                copy.wait_send()
            for copy in forwards(g, 1):
                copy.wait_recv()

        @pl.when(z < last_z)
        def _(g=g):
            for copy in forwards(g, 1):
                copy.wait_send()
            for copy in forwards(g, 0):
                copy.wait_recv()


def exchange(slc):
    rim_in = pl.pallas_call(
        pack_kernel,
        out_shape=jax.ShapeDtypeStruct((NDATE, 2, COLS), F32),
        name="pack",
    )(slc)
    return pl.pallas_call(
        exchange_kernel,
        out_shape=(
            jax.ShapeDtypeStruct((3, NDATE, 2, ROWS, COLS), F32),
            jax.ShapeDtypeStruct((3, NDATE, 2, COLS), F32),
        ),
        in_specs=[pl.BlockSpec(memory_space=pl.ANY)] * 2,
        out_specs=(pl.BlockSpec(memory_space=pl.ANY),) * 2,
        scratch_shapes=[
            pltpu.SemaphoreType.DMA((2,)),
            pltpu.SemaphoreType.DMA((2, 4, 8)),
            pltpu.SemaphoreType.DMA((2, 4, 8)),
            pltpu.SemaphoreType.DMA((2, 2, 4)),
            pltpu.SemaphoreType.DMA((2, 2, 4)),
        ],
        compiler_params=pltpu.CompilerParams(collective_id=0, has_side_effects=True),
        name="exchange",
    )(slc, rim_in)


WIN = 16
GROUPS = 17


def split(x):
    high = x.astype(BF16).astype(F32)
    return high, x - high


def date_vectors(offs_ref, axis):
    if axis == 0:
        row = iota((8, COLS), 0)
        out = []
        for part in range(4):
            vec = jnp.zeros((8, COLS), jnp.int32)
            for s in range(8):
                vec = jnp.where(row == s, offs_ref[0, part * 8 + s] + 2, vec)
            out.append(vec)
        return out
    lane = iota((8, COLS), 1) % NDATE
    vec = jnp.zeros((8, COLS), jnp.int32)
    row_vec = jnp.zeros((8, COLS), jnp.int32)
    for s in range(NDATE):
        vec = jnp.where(lane == s, offs_ref[1, s] + 2, vec)
        row_vec = jnp.where(lane == s, offs_ref[0, s] + 2, row_vec)
    return vec, row_vec


def mix_rows(rows, steps):
    bit0, bit1, bit2 = (steps & 1) != 0, (steps & 2) != 0, steps == 4
    one = [jnp.where(bit0, rows[i + 1], rows[i]) for i in range(22)]
    two = [jnp.where(bit1, one[i + 2], one[i]) for i in range(19)]
    base = [jnp.where(bit2, rows[i + 4], two[i]) for i in range(19)]
    return [
        0.5625 * (base[i + 1] + base[i + 2]) - 0.0625 * (base[i] + base[i + 3]) for i in range(WIN)
    ]


def link_kernel(
    pos_ref,
    offs_ref,
    main_ref,
    rim_ref,
    mask_ref,
    out_ref,
    eigen_ref,
    mixed,
    tall,
    rim_tall,
    keys,
    plain,
    sums,
    slots,
    vecs,
):
    date_pos, row_pos, last_date, last_row = (pos_ref[i] for i in range(4))
    lane8 = iota((8, COLS), 1)
    sub8 = iota((8, COLS), 0)

    row_steps = date_vectors(offs_ref, 0)
    col_steps, lane_row_steps = date_vectors(offs_ref, 1)
    for part in range(2):
        for eight in range(4):
            rows = []
            for i in range(23):
                slot, row = (i + 1) // 8, (i + 1) % 8
                start = ((slot * NDATE + eight * 8) * 2 + part) * ROWS + row
                x = main_ref[pl.ds(start, 8, stride=2 * ROWS), :]
                if slot == 0:
                    x = jnp.where(row_pos > 0, x, 0.0)
                if slot == 2:
                    x = jnp.where(row_pos < last_row, x, 0.0)
                rows.append(x)
            for i, x in enumerate(mix_rows(rows, row_steps[eight])):
                mixed[i, part * NDATE + eight * 8 : part * NDATE + eight * 8 + 8, :] = x

    for slot in range(3):
        x = jnp.concatenate([rim_ref[slot, :, 0, :], rim_ref[slot, :, 1, :]], axis=0)
        if slot == 0:
            x = jnp.where(row_pos > 0, x, 0.0)
        if slot == 2:
            x = jnp.where(row_pos < last_row, x, 0.0)
        rim_tall[slot] = jnp.concatenate([x, x], axis=0).T
    for side in range(2):
        rows = []
        for i in range(23):
            slot, row = (i + 1) // 8, (i + 1) % 8
            rows.append(rim_tall[slot, 16 * row + 8 * side : 16 * row + 8 * side + 8, :])
        done = mix_rows(rows, lane_row_steps)
        for m in range(8):
            tall[m, 136 * side : 136 * side + 8, :] = jnp.where(
                lane8 < PLANES, done[2 * m], done[2 * m + 1]
            )

    for m in range(8):
        tall[m, 8:136, :] = jnp.concatenate([mixed[2 * m], mixed[2 * m + 1]], axis=0).T
    for m in range(8):
        row = 8 * row_pos - 4 + 2 * m + (lane8 >= PLANES).astype(jnp.int32)
        inside = (row >= 0) & (row < 8 * (last_row + 1))
        weights = []
        for s in range(8):
            w = jnp.zeros((8, COLS), F32)
            for tap, value in enumerate((-0.0625, 0.5625, 0.5625, -0.0625)):
                w = jnp.where(col_steps + tap == s, value, w)
            weights.append(jnp.where(inside, w, 0.0))
        for g in range(GROUPS):
            x = weights[0] * tall[m, 8 * g + 1 : 8 * g + 9, :]
            for s in range(1, 8):
                x = x + weights[s] * tall[m, 8 * g + 1 + s : 8 * g + 9 + s, :]
            if g == 0:
                x = jnp.where((sub8 >= 4) | (date_pos > 0), x, 0.0)
            if g == GROUPS - 1:
                x = jnp.where((sub8 < 4) | (date_pos < last_date), x, 0.0)
            other = pltpu.roll(x, PLANES, 1)
            a = jnp.where(lane8 < PLANES, x, other)
            b = jnp.where(lane8 < PLANES, other, x)
            z = jnp.concatenate([a, b], axis=0)
            high, low = split(z)
            lane16 = iota((16, COLS), 1)
            first = g * COLS + 16 * m
            keys[first : first + 16, :] = jnp.where(lane16 < PLANES, high, low).astype(BF16)
            plain[first : first + 16, :] = z

    k_in = iota((COLS, COLS), 0) // NDATE % 2
    k_out = iota((COLS, COLS), 1) // PLANES
    adder = jnp.where(k_in == k_out, 1.0, 0.0).astype(BF16)
    for g in range(GROUPS):
        rows = slice(g * COLS, (g + 1) * COLS)
        total = jnp.dot(keys[rows, :], adder, preferred_element_type=F32)
        high, low = split(plain[rows, :] * total)
        sums[rows, :COLS] = high.astype(BF16)
        sums[rows, COLS:] = low.astype(BF16)

    population = jnp.zeros((8, COLS), jnp.int32)
    for w in range(5):
        population = population + lax.population_count(mask_ref[w])
    population = population.astype(F32)
    zero8 = jnp.zeros((8, COLS), jnp.int32)
    for r in range(8):
        pieces = []
        for n in range(WIN):
            i = n - r
            if 0 <= i <= 8:
                nine = (mask_ref[i // 2, r : r + 1, :] >> (9 * (i % 2))) & 511
                pieces.append(jnp.broadcast_to(nine, (8, COLS)))
            else:
                pieces.append(zero8)
        slots[r] = jnp.concatenate(pieces, axis=0).T

    across = lane8 % 8 - sub8
    shift0 = jnp.where(across >= 0, across, 31)
    shift1 = jnp.where(across <= 0, across + 8, 31)
    lane64 = iota((64, COLS), 1)
    quarter = lane64 // NDATE
    outer = (quarter == 0) | (quarter == 3)
    sign_a = jnp.where(quarter % 2 == 0, 1.0, -1.0)

    def one_block(blk, carry):
        q0 = pl.multiple_of(blk * COLS, COLS)
        c0 = pl.multiple_of(blk * 8, 8)
        near = keys[pl.ds(q0, 2 * COLS), :]
        bits = []
        for r in range(8):
            w = slots[r, pl.ds(c0, 8), :]
            bits.append(jnp.concatenate([(w >> shift0) & 1, (w >> shift1) & 1], axis=1))
        mask = jnp.concatenate(bits, axis=0).astype(F32)
        u = jnp.dot(mask.astype(BF16), sums[pl.ds(q0, 2 * COLS), :], preferred_element_type=F32)
        u = u[:, :COLS] + u[:, COLS:]
        same = jnp.where(lane64 < PLANES, u, pltpu.roll(u, PLANES, 1))
        cross = jnp.where(outer, pltpu.roll(u, 32, 1), pltpu.roll(u, 96, 1))
        v = same + sign_a * cross
        turned = sign_a * pltpu.roll(v, 32, 1)
        both = jnp.concatenate([v, turned], axis=0)
        high, low = split(both)
        left = jnp.concatenate([high, low], axis=1).astype(BF16)
        right = jnp.concatenate([near, near], axis=1)
        a = lax.dot_general(
            left, right, (((1,), (1,)), ((), ())), preferred_element_type=F32
        )
        a = a * jnp.concatenate([mask, mask], axis=0)
        high, low = split(a)
        c = jnp.dot(high.astype(BF16), near, preferred_element_type=F32) + jnp.dot(
            low.astype(BF16), near, preferred_element_type=F32
        )
        c = c + pltpu.roll(c, PLANES, 1)
        v2 = c[:64] - sign_a * pltpu.roll(c[64:], 32, 1)
        both = jnp.where(lane64 < PLANES, v2, v)
        for r in range(8):
            vecs[r, pl.ds(c0, 8), :] = both[8 * r : 8 * r + 8, :]
        return carry

    lax.fori_loop(0, 16, one_block, 0)

    for r in range(8):
        x = vecs[r].T
        pop = population[r : r + 1, :]
        inv = 1.0 / pop
        n1 = jnp.sum(x[PLANES:] * x[PLANES:], axis=0, keepdims=True) * (inv * inv)
        inv2 = inv * inv
        x2 = x[:PLANES] * inv2
        n2 = jnp.sum(x2 * x2, axis=0, keepdims=True)
        root2 = jnp.sqrt(n2 + EPSILON)
        root1 = jnp.sqrt(n1 + EPSILON)
        eigen_ref[r : r + 1, :] = root2 / root1
        out_ref[pl.ds(r, PLANES, stride=ROWS), :] = x2 * (jnp.sqrt(F32(NDATE)) / root2)


def link(pos, offsets, main, rim, masks):
    smem = pl.BlockSpec(memory_space=pltpu.SMEM)
    vmem = pl.BlockSpec(memory_space=pltpu.VMEM)
    linked, eigen = pl.pallas_call(
        link_kernel,
        out_shape=(
            jax.ShapeDtypeStruct((PLANES * ROWS, COLS), F32),
            jax.ShapeDtypeStruct((ROWS, COLS), F32),
        ),
        in_specs=[smem, smem, vmem, vmem, vmem],
        out_specs=(vmem, vmem),
        scratch_shapes=[
            pltpu.VMEM((WIN, PLANES, COLS), F32),
            pltpu.VMEM((8, 144, COLS), F32),
            pltpu.VMEM((3, COLS, COLS), F32),
            pltpu.VMEM((GROUPS * COLS, COLS), BF16),
            pltpu.VMEM((GROUPS * COLS, COLS), F32),
            pltpu.VMEM((GROUPS * COLS, 2 * COLS), BF16),
            pltpu.VMEM((8, COLS, COLS), jnp.int32),
            pltpu.VMEM((8, COLS, COLS), F32),
        ],
        compiler_params=pltpu.CompilerParams(vmem_limit_bytes=48 * 1024 * 1024),
        name="link",
    )(pos, offsets, main.reshape(-1, COLS), rim, masks)
    return linked.reshape(2, NDATE, ROWS, COLS), eigen


def on_device(slc, offsets, masks):
    main, rim = exchange(slc[:, 0])
    pos = jnp.stack(
        [
            lax.axis_index("date"),
            lax.axis_index("row"),
            jnp.int32(lax.axis_size("date") - 1),
            jnp.int32(lax.axis_size("row") - 1),
        ]
    ).astype(jnp.int32)
    return link(pos, offsets, main, rim, masks)


def solution(mesh):
    in_specs = (P(None, "date", "row", None), P(), P(None, "row", "date"))
    out_specs = (P(None, None, "row", "date"), P("row", "date"))
    return jax.shard_map(
        on_device, mesh=mesh, in_specs=in_specs, out_specs=out_specs, check_vma=False
    )
```

time: 385 us -> 41.9 us (0.11)
  the two profiles are of different devices: /device:TPU:39 before, /device:TPU:96 now
where the time goes in v1:
time: 41.9 us; the launch traced here: 41.2 us
  Pallas kernels  37.8 us (90%)
  local copies, waits for them, and re-layouts  2.69 us (6%)
  between operations  0.66 us (2%)
    pallas_call x1, Pallas kernels, exchange(): pl.pallas_call(exchange_kernel, out_shape=(jax.ShapeDtypeStruct((3, NDATE...  21.7 us
    pallas_call x1, Pallas kernels, link(): pl.pallas_call(link_kernel, out_shape=(jax.ShapeDtypeStruct((PLANES * ROW...  14.4 us
    unnamed x8, local copies, waits for them, and re-layouts  2.69 us
    pallas_call x1, Pallas kernels, exchange(): pl.pallas_call(pack_kernel, out_shape=jax.ShapeDtypeStruct((NDATE, 2, COL...  1.71 us

profile of v1, /device:TPU:96, one launch (start us, length us, event | category | flops | bytes accessed | tf_op | source)
XLA Modules:
  0.0 41.2 jit_solution(4112779427704226064)
XLA Ops:
  0.6 0.1 pad_add_fusion.pos_ref
  0.7 1.7 %pack.1.rim_in = f32[32,2,128]{2,1,0:T(2,128)} custom-call(f32[2,8,4096]{2,1,0:T(8,128)} %bitcast.6), custom_call_target="tpu_custom_call" | custom-call | tf_op jit(solution)/shard_map/pack/pallas_call | solution.py:157
  2.4 0.0 copy-start.2
  2.4 21.7 %exchange.1 = (f32[3,32,2,8,128]{4,3,2,1,0:T(8,128)}, f32[3,32,2,128]{3,2,1,0:T(2,128)}) custom-call(f32[2,8,4096]{2,1,0:T(8,128)} %bitcast.7, f32[32,2,128]{2,1,0:T(2,128)} %pack.1.rim_in), custom_call_target="tpu_custom_call" | custom-call | tf_op jit(solution)/shard_map/exchange/pallas_call | solution.py:162
  24.2 0.0 copy-start.3
  24.2 0.0 copy-done.2
  24.2 0.7 %copy-done.3 = s32[2,32]{1,0:T(2,128)S(1)} copy-done((s32[2,32]{1,0:T(2,128)S(1)}, s32[2,32]{1,0:T(2,128)}, u32[]{:S(2)}) %copy-start.3) | copy-done | bytes 280
  24.9 0.0 copy-start
  24.9 1.1 %copy-done = f32[3,32,2,8,128]{4,3,2,1,0:T(8,128)S(1)} copy-done((f32[3,32,2,8,128]{4,3,2,1,0:T(8,128)S(1)}, f32[3,32,2,8,128]{4,3,2,1,0:T(8,128)}, u32[]{:S(2)}) %copy-start) | copy-done | bytes 786456
  26.0 0.0 copy-start.1
  26.0 0.9 %copy-done.1 = f32[3,32,2,128]{3,2,1,0:T(2,128)S(1)} copy-done((f32[3,32,2,128]{3,2,1,0:T(2,128)S(1)}, f32[3,32,2,128]{3,2,1,0:T(2,128)}, u32[]{:S(2)}) %copy-start.1) | copy-done | bytes 98328
  26.9 14.4 %link.1 = (f32[512,128]{1,0:T(8,128)}, f32[8,128]{1,0:T(8,128)}) custom-call(s32[4]{0:T(128)S(1)} %pad_add_fusion.pos_ref, s32[2,32]{1,0:T(2,128)S(1)} %copy-done.3, f32[1536,128]{1,0:T(8,128)S(1)} %bitcast.5, f32[3,32,2,128]{3,2,1,0:T(2,128)S(1)} %copy-done.1, s32[5,8,128]{2,1,0:T(8,128)S(1)} %copy-done.2), custom_call_target="tpu_custom_call" | custom-call | tf_op jit(solution)/shard_map/link/pallas_call | solution.py:392
Async XLA Ops:
  2.4 21.8 %copy-start.2 = (s32[5,8,128]{2,1,0:T(8,128)S(1)}, s32[5,8,128]{2,1,0:T(8,128)}, u32[]{:S(2)}) copy-start(s32[5,8,128]{2,1,0:T(8,128)} %mask_ref.1) | copy-start | bytes 61444
  24.2 0.7 %copy-start.3 = (s32[2,32]{1,0:T(2,128)S(1)}, s32[2,32]{1,0:T(2,128)}, u32[]{:S(2)}) copy-start(s32[2,32]{1,0:T(2,128)} %offs_ref.1) | copy-start | bytes 772
  24.9 1.1 %copy-start = (f32[3,32,2,8,128]{4,3,2,1,0:T(8,128)S(1)}, f32[3,32,2,8,128]{4,3,2,1,0:T(8,128)}, u32[]{:S(2)}) copy-start(f32[3,32,2,8,128]{4,3,2,1,0:T(8,128)} %get-tuple-element.6) | copy-start | bytes 2359300
  26.0 0.9 %copy-start.1 = (f32[3,32,2,128]{3,2,1,0:T(2,128)S(1)}, f32[3,32,2,128]{3,2,1,0:T(2,128)}, u32[]{:S(2)}) copy-start(f32[3,32,2,128]{3,2,1,0:T(2,128)} %get-tuple-element.7.rim_ref) | copy-start | bytes 294916

commit v2 on v1

--- a/solution.py
+++ b/solution.py
@@ -370,7 +370,7 @@
             vecs[r, pl.ds(c0, 8), :] = both[8 * r : 8 * r + 8, :]
         return carry
 
-    lax.fori_loop(0, 16, one_block, 0)
+    lax.fori_loop(0, 16, one_block, 0, unroll=16)
 
     for r in range(8):
         x = vecs[r].T

time: 41.9 us -> 35.9 us (0.86)
  Pallas kernels: 37.8 us -> 31.8 us
    pallas_call x1, Pallas kernels: 14.4 us -> 8.4 us  [link(): pl.pallas_call(link_kernel, out_shape=(jax.ShapeDtypeStruct((PLANES * ROW...]
where the time goes in v2:
time: 35.9 us; the launch traced here: 35.3 us
  Pallas kernels  31.8 us (89%)
  local copies, waits for them, and re-layouts  2.69 us (7%)
  between operations  0.66 us (2%)
    pallas_call x1, Pallas kernels, exchange(): pl.pallas_call(exchange_kernel, out_shape=(jax.ShapeDtypeStruct((3, NDATE...  21.7 us
    pallas_call x1, Pallas kernels, link(): pl.pallas_call(link_kernel, out_shape=(jax.ShapeDtypeStruct((PLANES * ROW...  8.4 us
    unnamed x8, local copies, waits for them, and re-layouts  2.69 us
    pallas_call x1, Pallas kernels, exchange(): pl.pallas_call(pack_kernel, out_shape=jax.ShapeDtypeStruct((NDATE, 2, COL...  1.71 us

profile of v2, /device:TPU:96, one launch (start us, length us, event | category | flops | bytes accessed | tf_op | source)
XLA Modules:
  0.0 35.3 jit_solution(1950314342958383347)
XLA Ops:
  0.6 0.1 pad_add_fusion.pos_ref
  0.7 1.7 %pack.1.rim_in = f32[32,2,128]{2,1,0:T(2,128)} custom-call(f32[2,8,4096]{2,1,0:T(8,128)} %bitcast.6), custom_call_target="tpu_custom_call" | custom-call | tf_op jit(solution)/shard_map/pack/pallas_call | solution.py:157
  2.4 0.0 copy-start.2
  2.4 21.7 %exchange.1 = (f32[3,32,2,8,128]{4,3,2,1,0:T(8,128)}, f32[3,32,2,128]{3,2,1,0:T(2,128)}) custom-call(f32[2,8,4096]{2,1,0:T(8,128)} %bitcast.7, f32[32,2,128]{2,1,0:T(2,128)} %pack.1.rim_in), custom_call_target="tpu_custom_call" | custom-call | tf_op jit(solution)/shard_map/exchange/pallas_call | solution.py:162
  24.2 0.0 copy-start.3
  24.2 0.0 copy-done.2
  24.2 0.7 %copy-done.3 = s32[2,32]{1,0:T(2,128)S(1)} copy-done((s32[2,32]{1,0:T(2,128)S(1)}, s32[2,32]{1,0:T(2,128)}, u32[]{:S(2)}) %copy-start.3) | copy-done | bytes 280
  24.9 0.0 copy-start
  24.9 1.1 %copy-done = f32[3,32,2,8,128]{4,3,2,1,0:T(8,128)S(1)} copy-done((f32[3,32,2,8,128]{4,3,2,1,0:T(8,128)S(1)}, f32[3,32,2,8,128]{4,3,2,1,0:T(8,128)}, u32[]{:S(2)}) %copy-start) | copy-done | bytes 786456
  26.0 0.0 copy-start.1
  26.0 0.9 %copy-done.1 = f32[3,32,2,128]{3,2,1,0:T(2,128)S(1)} copy-done((f32[3,32,2,128]{3,2,1,0:T(2,128)S(1)}, f32[3,32,2,128]{3,2,1,0:T(2,128)}, u32[]{:S(2)}) %copy-start.1) | copy-done | bytes 98328
  26.9 8.4 %link.1 = (f32[512,128]{1,0:T(8,128)}, f32[8,128]{1,0:T(8,128)}) custom-call(s32[4]{0:T(128)S(1)} %pad_add_fusion.pos_ref, s32[2,32]{1,0:T(2,128)S(1)} %copy-done.3, f32[1536,128]{1,0:T(8,128)S(1)} %bitcast.5, f32[3,32,2,128]{3,2,1,0:T(2,128)S(1)} %copy-done.1, s32[5,8,128]{2,1,0:T(8,128)S(1)} %copy-done.2), custom_call_target="tpu_custom_call" | custom-call | tf_op jit(solution)/shard_map/link/pallas_call | solution.py:392
Async XLA Ops:
  2.4 21.8 %copy-start.2 = (s32[5,8,128]{2,1,0:T(8,128)S(1)}, s32[5,8,128]{2,1,0:T(8,128)}, u32[]{:S(2)}) copy-start(s32[5,8,128]{2,1,0:T(8,128)} %mask_ref.1) | copy-start | bytes 61444
  24.2 0.7 %copy-start.3 = (s32[2,32]{1,0:T(2,128)S(1)}, s32[2,32]{1,0:T(2,128)}, u32[]{:S(2)}) copy-start(s32[2,32]{1,0:T(2,128)} %offs_ref.1) | copy-start | bytes 772
  24.9 1.1 %copy-start = (f32[3,32,2,8,128]{4,3,2,1,0:T(8,128)S(1)}, f32[3,32,2,8,128]{4,3,2,1,0:T(8,128)}, u32[]{:S(2)}) copy-start(f32[3,32,2,8,128]{4,3,2,1,0:T(8,128)} %get-tuple-element.6) | copy-start | bytes 2359300
  26.0 0.9 %copy-start.1 = (f32[3,32,2,128]{3,2,1,0:T(2,128)S(1)}, f32[3,32,2,128]{3,2,1,0:T(2,128)}, u32[]{:S(2)}) copy-start(f32[3,32,2,128]{3,2,1,0:T(2,128)} %get-tuple-element.7.rim_ref) | copy-start | bytes 294916

commit v3 on v2

--- a/solution.py
+++ b/solution.py
@@ -1,5 +1,3 @@
-import functools
-
 import jax
 import jax.numpy as jnp
 from jax import lax
@@ -40,143 +38,14 @@
             rim_ref[dest, part : part + 1, :] = jnp.sum(spread, axis=0, keepdims=True)
 
 
-def pack_kernel(slc_ref, rim_ref):
-    pack_rim(slc_ref, rim_ref)
-
-
-def exchange_kernel(
-    slc_ref, rim_in, main_ref, rim_ref, own_sem, send_sem, recv_sem, fwd_send, fwd_recv
-):
-    me = lax.axis_index("date")
-    z = lax.axis_index("row")
-    last_z = lax.axis_size("row") - 1
-    block, place = me // 8, me % 8
-
-    barrier = pltpu.get_barrier_semaphore()
-    for s in range(1, NDATE):
-        pl.semaphore_signal(
-            barrier, inc=1, device_id={"date": (me + s) % NDATE}, device_id_type=MESH
-        )
-
-    for s in (1, last_z):
-        pl.semaphore_signal(
-            barrier, inc=1, device_id={"row": (z + s) % (last_z + 1)}, device_id_type=MESH
-        )
-    pl.semaphore_wait(barrier, NDATE + 1)
-
-    own = [
-        pltpu.make_async_copy(
-            slc_ref.at[:, :, pl.ds(pl.multiple_of(me * COLS, COLS), COLS)],
-            main_ref.at[1, me],
-            own_sem.at[0],
-        ),
-        pltpu.make_async_copy(rim_in.at[me], rim_ref.at[1, me], own_sem.at[1]),
-    ]
-    for copy in own:
-        copy.start()
-
-    sends = []
-    for g in range(4):
-        for j in range(8):
-            if g == 0 and j == 0:
-                continue
-            dest = ((block + g) % 4) * 8 + (place + j) % 8
-            for which, src, dst in (
-                (
-                    0,
-                    slc_ref.at[:, :, pl.ds(pl.multiple_of(dest * COLS, COLS), COLS)],
-                    main_ref.at[1, me],
-                ),
-                (1, rim_in.at[dest], rim_ref.at[1, me]),
-            ):
-                copy = pltpu.make_async_remote_copy(
-                    src_ref=src,
-                    dst_ref=dst,
-                    send_sem=send_sem.at[which, g, j],
-                    recv_sem=recv_sem.at[which, g, j],
-                    device_id={"date": dest},
-                    device_id_type=MESH,
-                )
-                copy.start()
-                sends.append((g, j, copy))
-
-    for copy in own:
-        copy.wait()
-
-    def forwards(g, side):
-        group = (block + 4 - g) % 4
-        slot, to = (2, z - 1) if side == 0 else (0, z + 1)
-        first = pl.multiple_of(group * 8, 8)
-        return [
-            pltpu.make_async_remote_copy(
-                src_ref=ref.at[1, pl.ds(first, 8)],
-                dst_ref=ref.at[slot, pl.ds(first, 8)],
-                send_sem=fwd_send.at[which, side, g],
-                recv_sem=fwd_recv.at[which, side, g],
-                device_id={"row": to},
-                device_id_type=MESH,
-            )
-            for which, ref in ((0, main_ref), (1, rim_ref))
-        ]
-
-    for g in range(4):
-        for step, _, copy in sends:
-            if step == g:
-                copy.wait_recv()
-
-        @pl.when(z > 0)
-        def _(g=g):
-            for copy in forwards(g, 0):
-                copy.start()
-
-        @pl.when(z < last_z)
-        def _(g=g):
-            for copy in forwards(g, 1):
-                copy.start()
-
-    for _, _, copy in sends:
-        copy.wait_send()
-    for g in range(4):
-
-        @pl.when(z > 0)
-        def _(g=g):
-            for copy in forwards(g, 0):
-                copy.wait_send()
-            for copy in forwards(g, 1):
-                copy.wait_recv()
-
-        @pl.when(z < last_z)
-        def _(g=g):
-            for copy in forwards(g, 1):
-                copy.wait_send()
-            for copy in forwards(g, 0):
-                copy.wait_recv()
-
-
-def exchange(slc):
-    rim_in = pl.pallas_call(
-        pack_kernel,
-        out_shape=jax.ShapeDtypeStruct((NDATE, 2, COLS), F32),
-        name="pack",
-    )(slc)
-    return pl.pallas_call(
-        exchange_kernel,
-        out_shape=(
-            jax.ShapeDtypeStruct((3, NDATE, 2, ROWS, COLS), F32),
-            jax.ShapeDtypeStruct((3, NDATE, 2, COLS), F32),
-        ),
-        in_specs=[pl.BlockSpec(memory_space=pl.ANY)] * 2,
-        out_specs=(pl.BlockSpec(memory_space=pl.ANY),) * 2,
-        scratch_shapes=[
-            pltpu.SemaphoreType.DMA((2,)),
-            pltpu.SemaphoreType.DMA((2, 4, 8)),
-            pltpu.SemaphoreType.DMA((2, 4, 8)),
-            pltpu.SemaphoreType.DMA((2, 2, 4)),
-            pltpu.SemaphoreType.DMA((2, 2, 4)),
-        ],
-        compiler_params=pltpu.CompilerParams(collective_id=0, has_side_effects=True),
-        name="exchange",
-    )(slc, rim_in)
+NEAR_LAST = sorted(
+    ((g, j) for g in range(4) for j in range(8) if (g, j) != (0, 0)),
+    key=lambda s: -(min(s[0], 4 - s[0]) + min(s[1] // 2, 4 - s[1] // 2)),
+)
+
+
+def peer(date, g, j):
+    return (date // 8 + g) % 4 * 8 + (date % 8 + j) % 8
 
 
 WIN = 16
@@ -217,14 +86,16 @@
     ]
 
 
-def link_kernel(
-    pos_ref,
+def kernel(
     offs_ref,
-    main_ref,
-    rim_ref,
+    slc_ref,
     mask_ref,
     out_ref,
     eigen_ref,
+    slc_here,
+    rim_here,
+    main_ref,
+    rim_ref,
     mixed,
     tall,
     rim_tall,
@@ -233,11 +104,131 @@
     sums,
     slots,
     vecs,
+    own_sem,
+    send_sem,
+    recv_sem,
+    fwd_send,
+    fwd_recv,
 ):
-    date_pos, row_pos, last_date, last_row = (pos_ref[i] for i in range(4))
+    date_pos, row_pos = lax.axis_index("date"), lax.axis_index("row")
+    last_date, last_row = lax.axis_size("date") - 1, lax.axis_size("row") - 1
     lane8 = iota((8, COLS), 1)
     sub8 = iota((8, COLS), 0)
 
+    load = pltpu.make_async_copy(slc_ref, slc_here, own_sem.at[2])
+    load.start()
+    barrier = pltpu.get_barrier_semaphore()
+    for g, j in NEAR_LAST:
+        pl.semaphore_signal(
+            barrier, inc=1, device_id={"date": peer(date_pos, g, j)}, device_id_type=MESH
+        )
+    for s in (1, last_row):
+        pl.semaphore_signal(
+            barrier, inc=1, device_id={"row": (row_pos + s) % (last_row + 1)}, device_id_type=MESH
+        )
+
+    load.wait()
+    pack_rim(slc_here, rim_here)
+
+    population = jnp.zeros((8, COLS), jnp.int32)
+    for w in range(5):
+        population = population + lax.population_count(mask_ref[w])
+    population = population.astype(F32)
+    zero8 = jnp.zeros((8, COLS), jnp.int32)
+    for r in range(8):
+        pieces = []
+        for n in range(WIN):
+            i = n - r
+            if 0 <= i <= 8:
+                nine = (mask_ref[i // 2, r : r + 1, :] >> (9 * (i % 2))) & 511
+                pieces.append(jnp.broadcast_to(nine, (8, COLS)))
+            else:
+                pieces.append(zero8)
+        slots[r] = jnp.concatenate(pieces, axis=0).T
+
+    pl.semaphore_wait(barrier, NDATE + 1)
+
+    def part(which, date):
+        return (
+            (slc_ref.at[:, :, pl.ds(pl.multiple_of(date * COLS, COLS), COLS)], main_ref)
+            if which == 0
+            else (rim_here.at[date], rim_ref)
+        )
+
+    sends = {}
+    for g, j in NEAR_LAST:
+        dest = peer(date_pos, g, j)
+        for which in range(2):
+            src, ref = part(which, dest)
+            copy = pltpu.make_async_remote_copy(
+                src_ref=src,
+                dst_ref=ref.at[1, date_pos],
+                send_sem=send_sem.at[which, g, j],
+                recv_sem=recv_sem.at[which, g, j],
+                device_id={"date": dest},
+                device_id_type=MESH,
+            )
+            copy.start()
+            sends[which, g, j] = copy
+    own = []
+    for which in range(2):
+        src, ref = part(which, date_pos)
+        own.append(pltpu.make_async_copy(src, ref.at[1, date_pos], own_sem.at[which]))
+    for copy in own:
+        copy.start()
+
+    def forwards(g, side):
+        first = pl.multiple_of((date_pos // 8 + 4 - g) % 4 * 8, 8)
+        slot, to = (2, row_pos - 1) if side == 0 else (0, row_pos + 1)
+        return [
+            pltpu.make_async_remote_copy(
+                src_ref=ref.at[1, pl.ds(first, 8)],
+                dst_ref=ref.at[slot, pl.ds(first, 8)],
+                send_sem=fwd_send.at[which, side, g],
+                recv_sem=fwd_recv.at[which, side, g],
+                device_id={"row": to},
+                device_id_type=MESH,
+            )
+            for which, ref in ((0, main_ref), (1, rim_ref))
+        ]
+
+    for copy in own:
+        copy.wait()
+    for g in (0, 1, 3, 2):
+        for j in range(8):
+            for which in range(2):
+                if (which, g, j) in sends:
+                    sends[which, g, j].wait_recv()
+
+        @pl.when(row_pos > 0)
+        def _(g=g):
+            for copy in forwards(g, 0):
+                copy.start()
+
+        @pl.when(row_pos < last_row)
+        def _(g=g):
+            for copy in forwards(g, 1):
+                copy.start()
+
+    for copy in sends.values():
+        copy.wait_send()
+    for g in (0, 1, 3, 2):
+
+        @pl.when(row_pos > 0)
+        def _(g=g):
+            for copy in forwards(g, 0):
+                copy.wait_send()
+            for copy in forwards(g, 1):
+                copy.wait_recv()
+
+        @pl.when(row_pos < last_row)
+        def _(g=g):
+            for copy in forwards(g, 1):
+                copy.wait_send()
+            for copy in forwards(g, 0):
+                copy.wait_recv()
+
+    main_rows = main_ref.reshape(-1, COLS)
     row_steps = date_vectors(offs_ref, 0)
     col_steps, lane_row_steps = date_vectors(offs_ref, 1)
     for part in range(2):
@@ -246,7 +237,7 @@
             for i in range(23):
                 slot, row = (i + 1) // 8, (i + 1) % 8
                 start = ((slot * NDATE + eight * 8) * 2 + part) * ROWS + row
-                x = main_ref[pl.ds(start, 8, stride=2 * ROWS), :]
+                x = main_rows[pl.ds(start, 8, stride=2 * ROWS), :]
                 if slot == 0:
                     x = jnp.where(row_pos > 0, x, 0.0)
                 if slot == 2:
@@ -311,22 +302,6 @@
         high, low = split(plain[rows, :] * total)
         sums[rows, :COLS] = high.astype(BF16)
         sums[rows, COLS:] = low.astype(BF16)
-
-    population = jnp.zeros((8, COLS), jnp.int32)
-    for w in range(5):
-        population = population + lax.population_count(mask_ref[w])
-    population = population.astype(F32)
-    zero8 = jnp.zeros((8, COLS), jnp.int32)
-    for r in range(8):
-        pieces = []
-        for n in range(WIN):
-            i = n - r
-            if 0 <= i <= 8:
-                nine = (mask_ref[i // 2, r : r + 1, :] >> (9 * (i % 2))) & 511
-                pieces.append(jnp.broadcast_to(nine, (8, COLS)))
-            else:
-                pieces.append(zero8)
-        slots[r] = jnp.concatenate(pieces, axis=0).T
 
     across = lane8 % 8 - sub8
     shift0 = jnp.where(across >= 0, across, 31)
@@ -386,18 +361,22 @@
         out_ref[pl.ds(r, PLANES, stride=ROWS), :] = x2 * (jnp.sqrt(F32(NDATE)) / root2)
 
 
-def link(pos, offsets, main, rim, masks):
+def on_device(slc, offsets, masks):
     smem = pl.BlockSpec(memory_space=pltpu.SMEM)
     vmem = pl.BlockSpec(memory_space=pltpu.VMEM)
     linked, eigen = pl.pallas_call(
-        link_kernel,
+        kernel,
         out_shape=(
             jax.ShapeDtypeStruct((PLANES * ROWS, COLS), F32),
             jax.ShapeDtypeStruct((ROWS, COLS), F32),
         ),
-        in_specs=[smem, smem, vmem, vmem, vmem],
+        in_specs=[smem, pl.BlockSpec(memory_space=pl.ANY), vmem],
         out_specs=(vmem, vmem),
         scratch_shapes=[
+            pltpu.VMEM((2, ROWS, NDATE * COLS), F32),
+            pltpu.VMEM((NDATE, 2, COLS), F32),
+            pltpu.VMEM((3, NDATE, 2, ROWS, COLS), F32),
+            pltpu.VMEM((3, NDATE, 2, COLS), F32),
             pltpu.VMEM((WIN, PLANES, COLS), F32),
             pltpu.VMEM((8, 144, COLS), F32),
             pltpu.VMEM((3, COLS, COLS), F32),
@@ -406,24 +385,18 @@
             pltpu.VMEM((GROUPS * COLS, 2 * COLS), BF16),
             pltpu.VMEM((8, COLS, COLS), jnp.int32),
             pltpu.VMEM((8, COLS, COLS), F32),
+            pltpu.SemaphoreType.DMA((3,)),
+            pltpu.SemaphoreType.DMA((2, 4, 8)),
+            pltpu.SemaphoreType.DMA((2, 4, 8)),
+            pltpu.SemaphoreType.DMA((2, 2, 4)),
+            pltpu.SemaphoreType.DMA((2, 2, 4)),
         ],
-        compiler_params=pltpu.CompilerParams(vmem_limit_bytes=48 * 1024 * 1024),
-        name="link",
-    )(pos, offsets, main.reshape(-1, COLS), rim, masks)
+        compiler_params=pltpu.CompilerParams(
+            collective_id=0, has_side_effects=True, vmem_limit_bytes=48 * 1024 * 1024
+        ),
+        name="phase_linking",
+    )(offsets, slc[:, 0], masks)
     return linked.reshape(2, NDATE, ROWS, COLS), eigen
-
-
-def on_device(slc, offsets, masks):
-    main, rim = exchange(slc[:, 0])
-    pos = jnp.stack(
-        [
-            lax.axis_index("date"),
-            lax.axis_index("row"),
-            jnp.int32(lax.axis_size("date") - 1),
-            jnp.int32(lax.axis_size("row") - 1),
-        ]
-    ).astype(jnp.int32)
-    return link(pos, offsets, main, rim, masks)
 
 
 def solution(mesh):

time: 35.9 us -> 34.9 us (0.972); the launches traced: 35.3 us -> 34.7 us
  Pallas kernels: 31.8 us -> 30.4 us
  local copies, waits for them, and re-layouts: 2.69 us -> 3.65 us
    pallas_call x3 -> x1, Pallas kernels: 31.8 us -> 30.4 us  [on_device(): pl.pallas_call(kernel, out_shape=(jax.ShapeDtypeStruct((PLANES * ROWS, CO...]
    unnamed x8, local copies, waits for them, and re-layouts: 2.69 us -> 3.65 us
where the time goes in v3:
time: 34.9 us; the launch traced here: 34.7 us
  Pallas kernels  30.4 us (87%)
  local copies, waits for them, and re-layouts  3.65 us (10%)
  between operations  0.65 us (2%)
    pallas_call x1, Pallas kernels, on_device(): pl.pallas_call(kernel, out_shape=(jax.ShapeDtypeStruct((PLANES * ROWS, CO...  30.4 us
    unnamed x8, local copies, waits for them, and re-layouts  3.65 us

profile of v3, /device:TPU:96, one launch (start us, length us, event | category | flops | bytes accessed | tf_op | source)
XLA Modules:
  0.0 34.7 jit_solution(2843733936812324180)
XLA Ops:
  0.6 0.0 copy-start.2
  0.6 0.7 %copy-done.2 = s32[2,32]{1,0:T(2,128)S(1)} copy-done((s32[2,32]{1,0:T(2,128)S(1)}, s32[2,32]{1,0:T(2,128)}, u32[]{:S(2)}) %copy-start.2) | copy-done | bytes 280
  1.3 0.0 copy-start
  1.3 0.9 %copy-done = f32[2,1,8,4096]{3,2,1,0:T(8,128)S(1)} copy-done((f32[2,1,8,4096]{3,2,1,0:T(8,128)S(1)}, f32[2,1,8,4096]{3,2,1,0:T(8,128)}, u32[]{:S(2)}) %copy-start) | copy-done | bytes 262168
  2.3 0.0 copy-start.1
  2.3 0.7 %copy-done.1 = s32[5,8,128]{2,1,0:T(8,128)S(1)} copy-done((s32[5,8,128]{2,1,0:T(8,128)S(1)}, s32[5,8,128]{2,1,0:T(8,128)}, u32[]{:S(2)}) %copy-start.1) | copy-done | bytes 20504
  3.0 30.4 %phase_linking.1 = (f32[512,128]{1,0:T(8,128)S(1)}, f32[8,128]{1,0:T(8,128)S(1)}) custom-call(s32[2,32]{1,0:T(2,128)S(1)} %copy-done.2, f32[2,8,4096]{2,1,0:T(8,128)S(1)} %bitcast.2, s32[5,8,128]{2,1,0:T(8,128)S(1)} %copy-done.1), custom_call_target="tpu_custom_call" | custom-call | tf_op jit(solution)/shard_map/phase_linking/pallas_call | solution.py:367
  33.4 0.7 %copy.7 = f32[2,32,8,128]{3,2,1,0:T(8,128)} copy(f32[2,32,8,128]{3,2,1,0:T(8,128)S(1)} %bitcast.3) | data formatting | bytes 524288
  34.1 0.6 %copy.8 = f32[8,128]{1,0:T(8,128)} copy(f32[8,128]{1,0:T(8,128)S(1)} %get-tuple-element.9) | data formatting | bytes 8192
Async XLA Ops:
  0.6 0.7 %copy-start.2 = (s32[2,32]{1,0:T(2,128)S(1)}, s32[2,32]{1,0:T(2,128)}, u32[]{:S(2)}) copy-start(s32[2,32]{1,0:T(2,128)} %offs_ref.1) | copy-start | bytes 772
  1.3 0.9 %copy-start = (f32[2,1,8,4096]{3,2,1,0:T(8,128)S(1)}, f32[2,1,8,4096]{3,2,1,0:T(8,128)}, u32[]{:S(2)}) copy-start(f32[2,1,8,4096]{3,2,1,0:T(8,128)} %param.3) | copy-start | bytes 786436
  2.3 0.7 %copy-start.1 = (s32[5,8,128]{2,1,0:T(8,128)S(1)}, s32[5,8,128]{2,1,0:T(8,128)}, u32[]{:S(2)}) copy-start(s32[5,8,128]{2,1,0:T(8,128)} %mask_ref.1) | copy-start | bytes 61444

commit v4 on v3

--- a/solution.py
+++ b/solution.py
@@ -38,14 +38,16 @@
             rim_ref[dest, part : part + 1, :] = jnp.sum(spread, axis=0, keepdims=True)
 
 
-NEAR_LAST = sorted(
-    ((g, j) for g in range(4) for j in range(8) if (g, j) != (0, 0)),
-    key=lambda s: -(min(s[0], 4 - s[0]) + min(s[1] // 2, 4 - s[1] // 2)),
-)
-
-
-def peer(date, g, j):
-    return (date // 8 + g) % 4 * 8 + (date % 8 + j) % 8
+def hops(step):
+    return min(step[0], 4 - step[0]) + min(step[1], 4 - step[1])
+
+
+CHIPS = sorted(((g, i) for g in range(4) for i in range(4)), key=hops)
+SENDS = [(g, i, k) for g, i in CHIPS for k in range(2) if (g, i, k) != (0, 0, 0)]
+
+
+def peer(date, g, i, k):
+    return (date // 8 + g) % 4 * 8 + (date // 2 + i) % 4 * 2 + (date + k) % 2
 
 
 WIN = 16
@@ -87,11 +89,13 @@
 
 
 def kernel(
-    offs_ref,
+    offs_in,
     slc_ref,
-    mask_ref,
+    mask_in,
     out_ref,
     eigen_ref,
+    offs_ref,
+    mask_ref,
     slc_here,
     rim_here,
     main_ref,
@@ -116,19 +120,25 @@
     sub8 = iota((8, COLS), 0)
 
     load = pltpu.make_async_copy(slc_ref, slc_here, own_sem.at[2])
+    load_mask = pltpu.make_async_copy(mask_in, mask_ref, own_sem.at[3])
+    load_offs = pltpu.make_async_copy(offs_in, offs_ref, own_sem.at[4])
     load.start()
+    load_mask.start()
+    load_offs.start()
     barrier = pltpu.get_barrier_semaphore()
-    for g, j in NEAR_LAST:
-        pl.semaphore_signal(
-            barrier, inc=1, device_id={"date": peer(date_pos, g, j)}, device_id_type=MESH
-        )
     for s in (1, last_row):
         pl.semaphore_signal(
             barrier, inc=1, device_id={"row": (row_pos + s) % (last_row + 1)}, device_id_type=MESH
         )
+    for g, i, k in SENDS[::-1]:
+        pl.semaphore_signal(
+            barrier, inc=1, device_id={"date": peer(date_pos, g, i, k)}, device_id_type=MESH
+        )
 
     load.wait()
     pack_rim(slc_here, rim_here)
+    load_mask.wait()
+    load_offs.wait()
 
     population = jnp.zeros((8, COLS), jnp.int32)
     for w in range(5):
@@ -150,83 +160,91 @@
 
     def part(which, date):
         return (
-            (slc_ref.at[:, :, pl.ds(pl.multiple_of(date * COLS, COLS), COLS)], main_ref)
+            (slc_here.at[:, :, pl.ds(pl.multiple_of(date * COLS, COLS), COLS)], main_ref)
             if which == 0
             else (rim_here.at[date], rim_ref)
         )
 
-    sends = {}
-    for g, j in NEAR_LAST:
-        dest = peer(date_pos, g, j)
-        for which in range(2):
-            src, ref = part(which, dest)
-            copy = pltpu.make_async_remote_copy(
-                src_ref=src,
-                dst_ref=ref.at[1, date_pos],
-                send_sem=send_sem.at[which, g, j],
-                recv_sem=recv_sem.at[which, g, j],
-                device_id={"date": dest},
-                device_id_type=MESH,
-            )
-            copy.start()
-            sends[which, g, j] = copy
+    def send(which, g, i, k):
+        dest = peer(date_pos, g, i, k)
+        src, ref = part(which, dest)
+        return pltpu.make_async_remote_copy(
+            src_ref=src,
+            dst_ref=ref.at[1, date_pos],
+            send_sem=send_sem.at[which, g, 2 * i + k],
+            recv_sem=recv_sem.at[which, g, 2 * i + k],
+            device_id={"date": dest},
+            device_id_type=MESH,
+        )
+
+    mains = {step: send(0, *step) for step in SENDS}
+    rims = {step: send(1, *step) for step in SENDS}
+    for copy in mains.values():
+        copy.start()
     own = []
     for which in range(2):
         src, ref = part(which, date_pos)
         own.append(pltpu.make_async_copy(src, ref.at[1, date_pos], own_sem.at[which]))
     for copy in own:
         copy.start()
-
-    def forwards(g, side):
-        first = pl.multiple_of((date_pos // 8 + 4 - g) % 4 * 8, 8)
+    for copy in rims.values():
+        copy.start()
+
+    def forward(side, number, first, count, ref):
         slot, to = (2, row_pos - 1) if side == 0 else (0, row_pos + 1)
-        return [
-            pltpu.make_async_remote_copy(
-                src_ref=ref.at[1, pl.ds(first, 8)],
-                dst_ref=ref.at[slot, pl.ds(first, 8)],
-                send_sem=fwd_send.at[which, side, g],
-                recv_sem=fwd_recv.at[which, side, g],
-                device_id={"row": to},
-                device_id_type=MESH,
-            )
-            for which, ref in ((0, main_ref), (1, rim_ref))
-        ]
-
-    for copy in own:
-        copy.wait()
-    for g in (0, 1, 3, 2):
-        for j in range(8):
-            for which in range(2):
-                if (which, g, j) in sends:
-                    sends[which, g, j].wait_recv()
+        return pltpu.make_async_remote_copy(
+            src_ref=ref.at[1, pl.ds(first, count)],
+            dst_ref=ref.at[slot, pl.ds(first, count)],
+            send_sem=fwd_send.at[side, number],
+            recv_sem=fwd_recv.at[side, number],
+            device_id={"row": to},
+            device_id_type=MESH,
+        )
+
+    def forwards(side):
+        out = []
+        for number, (g, i) in enumerate(CHIPS):
+            first = (date_pos // 8 + 4 - g) % 4 * 8 + (date_pos // 2 + 4 - i) % 4 * 2
+            out.append(forward(side, number, first, 2, main_ref))
+        return out + [forward(side, len(CHIPS), 0, NDATE, rim_ref)]
+
+    before, after = forwards(0), forwards(1)
+    for number in range(len(CHIPS) + 1):
+        if number < len(CHIPS):
+            g, i = CHIPS[number]
+            for k in range(2):
+                if (g, i, k) in mains:
+                    mains[g, i, k].wait_recv()
+                else:
+                    own[0].wait()
+        else:
+            own[1].wait()
+            for copy in rims.values():
+                copy.wait_recv()
 
         @pl.when(row_pos > 0)
-        def _(g=g):
-            for copy in forwards(g, 0):
-                copy.start()
+        def _(number=number):
+            before[number].start()
 
         @pl.when(row_pos < last_row)
-        def _(g=g):
-            for copy in forwards(g, 1):
-                copy.start()
-
-    for copy in sends.values():
-        copy.wait_send()
-    for g in (0, 1, 3, 2):
-
-        @pl.when(row_pos > 0)
-        def _(g=g):
-            for copy in forwards(g, 0):
-                copy.wait_send()
-            for copy in forwards(g, 1):
-                copy.wait_recv()
-
-        @pl.when(row_pos < last_row)
-        def _(g=g):
-            for copy in forwards(g, 1):
-                copy.wait_send()
-            for copy in forwards(g, 0):
-                copy.wait_recv()
+        def _(number=number):
+            after[number].start()
+
+    for step in SENDS:
+        mains[step].wait_send()
+        rims[step].wait_send()
+
+    @pl.when(row_pos > 0)
+    def _():
+        for number in range(len(CHIPS) + 1):
+            before[number].wait_send()
+            after[number].wait_recv()
+
+    @pl.when(row_pos < last_row)
+    def _():
+        for number in range(len(CHIPS) + 1):
+            after[number].wait_send()
+            before[number].wait_recv()
 
     main_rows = main_ref.reshape(-1, COLS)
     row_steps = date_vectors(offs_ref, 0)
@@ -362,7 +380,7 @@
 
 
 def on_device(slc, offsets, masks):
-    smem = pl.BlockSpec(memory_space=pltpu.SMEM)
+    hbm = pl.BlockSpec(memory_space=pltpu.HBM)
     vmem = pl.BlockSpec(memory_space=pltpu.VMEM)
     linked, eigen = pl.pallas_call(
         kernel,
@@ -370,9 +388,11 @@
             jax.ShapeDtypeStruct((PLANES * ROWS, COLS), F32),
             jax.ShapeDtypeStruct((ROWS, COLS), F32),
         ),
-        in_specs=[smem, pl.BlockSpec(memory_space=pl.ANY), vmem],
+        in_specs=[hbm, hbm, hbm],
         out_specs=(vmem, vmem),
         scratch_shapes=[
+            pltpu.SMEM((2, NDATE), jnp.int32),
+            pltpu.VMEM((5, ROWS, COLS), jnp.int32),
             pltpu.VMEM((2, ROWS, NDATE * COLS), F32),
             pltpu.VMEM((NDATE, 2, COLS), F32),
             pltpu.VMEM((3, NDATE, 2, ROWS, COLS), F32),
@@ -385,17 +405,17 @@
             pltpu.VMEM((GROUPS * COLS, 2 * COLS), BF16),
             pltpu.VMEM((8, COLS, COLS), jnp.int32),
             pltpu.VMEM((8, COLS, COLS), F32),
-            pltpu.SemaphoreType.DMA((3,)),
+            pltpu.SemaphoreType.DMA((5,)),
             pltpu.SemaphoreType.DMA((2, 4, 8)),
             pltpu.SemaphoreType.DMA((2, 4, 8)),
-            pltpu.SemaphoreType.DMA((2, 2, 4)),
-            pltpu.SemaphoreType.DMA((2, 2, 4)),
+            pltpu.SemaphoreType.DMA((2, 17)),
+            pltpu.SemaphoreType.DMA((2, 17)),
         ],
         compiler_params=pltpu.CompilerParams(
             collective_id=0, has_side_effects=True, vmem_limit_bytes=48 * 1024 * 1024
         ),
         name="phase_linking",
-    )(offsets, slc[:, 0], masks)
+    )(*(pltpu.with_memory_space_constraint(x, pltpu.HBM) for x in (offsets, slc[:, 0], masks)))
     return linked.reshape(2, NDATE, ROWS, COLS), eigen
 
 

time: 34.9 us -> 29.8 us (0.85)
  Pallas kernels: 30.4 us -> 27.8 us
  local copies, waits for them, and re-layouts: 3.65 us -> 1.3 us
    pallas_call x1, Pallas kernels: 30.4 us -> 27.8 us  [on_device(): pl.pallas_call(kernel, out_shape=(jax.ShapeDtypeStruct((PLANES * ROWS, CO...]
    unnamed x8 -> x2, local copies, waits for them, and re-layouts: 3.65 us -> 1.3 us
where the time goes in v4:
time: 29.8 us; the launch traced here: 29.7 us
  Pallas kernels  27.8 us (93%)
  local copies, waits for them, and re-layouts  1.3 us (4%)
  between operations  0.64 us (2%)
    pallas_call x1, Pallas kernels, on_device(): pl.pallas_call(kernel, out_shape=(jax.ShapeDtypeStruct((PLANES * ROWS, CO...  27.8 us
    unnamed x2, local copies, waits for them, and re-layouts  1.3 us

profile of v4, /device:TPU:96, one launch (start us, length us, event | category | flops | bytes accessed | tf_op | source)
XLA Modules:
  0.0 29.7 jit_solution(7131856445526642134)
XLA Ops:
  0.6 27.8 %phase_linking.1 = (f32[512,128]{1,0:T(8,128)S(1)}, f32[8,128]{1,0:T(8,128)S(1)}) custom-call(s32[2,32]{1,0:T(2,128)} %offs_in.1, f32[2,8,4096]{2,1,0:T(8,128)} %bitcast.3, s32[5,8,128]{2,1,0:T(8,128)} %mask_in.1), custom_call_target="tpu_custom_call" | custom-call | tf_op jit(solution)/shard_map/phase_linking/pallas_call | solution.py:385
  28.4 0.7 %copy.7 = f32[2,32,8,128]{3,2,1,0:T(8,128)} copy(f32[2,32,8,128]{3,2,1,0:T(8,128)S(1)} %bitcast.2) | data formatting | bytes 524288
  29.1 0.6 %copy.8 = f32[8,128]{1,0:T(8,128)} copy(f32[8,128]{1,0:T(8,128)S(1)} %get-tuple-element.9) | data formatting | bytes 8192

commit v5 on v4

--- a/solution.py
+++ b/solution.py
@@ -329,16 +329,19 @@
     outer = (quarter == 0) | (quarter == 3)
     sign_a = jnp.where(quarter % 2 == 0, 1.0, -1.0)
 
-    def one_block(blk, carry):
-        q0 = pl.multiple_of(blk * COLS, COLS)
-        c0 = pl.multiple_of(blk * 8, 8)
-        near = keys[pl.ds(q0, 2 * COLS), :]
+    def first(blk):
+        q0 = blk * COLS
         bits = []
         for r in range(8):
-            w = slots[r, pl.ds(c0, 8), :]
+            w = slots[r, blk * 8 : blk * 8 + 8, :]
             bits.append(jnp.concatenate([(w >> shift0) & 1, (w >> shift1) & 1], axis=1))
         mask = jnp.concatenate(bits, axis=0).astype(F32)
-        u = jnp.dot(mask.astype(BF16), sums[pl.ds(q0, 2 * COLS), :], preferred_element_type=F32)
+        u = jnp.dot(mask.astype(BF16), sums[q0 : q0 + 2 * COLS, :], preferred_element_type=F32)
+        return mask, u
+
+    def second(blk, u):
+        q0 = blk * COLS
+        near = keys[q0 : q0 + 2 * COLS, :]
         u = u[:, :COLS] + u[:, COLS:]
         same = jnp.where(lane64 < PLANES, u, pltpu.roll(u, PLANES, 1))
         cross = jnp.where(outer, pltpu.roll(u, 32, 1), pltpu.roll(u, 96, 1))
@@ -351,19 +354,30 @@
         a = lax.dot_general(
             left, right, (((1,), (1,)), ((), ())), preferred_element_type=F32
         )
+        return v, a
+
+    def third(blk, mask, a):
+        q0 = blk * COLS
+        near = keys[q0 : q0 + 2 * COLS, :]
         a = a * jnp.concatenate([mask, mask], axis=0)
         high, low = split(a)
-        c = jnp.dot(high.astype(BF16), near, preferred_element_type=F32) + jnp.dot(
-            low.astype(BF16), near, preferred_element_type=F32
-        )
+        both = jnp.concatenate([high.astype(BF16), low.astype(BF16)], axis=0)
+        return jnp.dot(both, near, preferred_element_type=F32)
+
+    def fourth(blk, v, c):
+        c = c[:128] + c[128:]
         c = c + pltpu.roll(c, PLANES, 1)
         v2 = c[:64] - sign_a * pltpu.roll(c[64:], 32, 1)
         both = jnp.where(lane64 < PLANES, v2, v)
         for r in range(8):
-            vecs[r, pl.ds(c0, 8), :] = both[8 * r : 8 * r + 8, :]
-        return carry
-
-    lax.fori_loop(0, 16, one_block, 0, unroll=16)
+            vecs[r, blk * 8 : blk * 8 + 8, :] = both[8 * r : 8 * r + 8, :]
+
+    blocks = range(16)
+    ones = [first(b) for b in blocks]
+    twos = [second(b, ones[b][1]) for b in blocks]
+    threes = [third(b, ones[b][0], twos[b][1]) for b in blocks]
+    for b in blocks:
+        fourth(b, twos[b][0], threes[b])
 
     for r in range(8):
         x = vecs[r].T

time: 29.8 us -> 26 us (0.87)
  Pallas kernels: 27.8 us -> 24 us
    pallas_call x1, Pallas kernels: 27.8 us -> 24 us  [on_device(): pl.pallas_call(kernel, out_shape=(jax.ShapeDtypeStruct((PLANES * ROWS, CO...]
where the time goes in v5:
time: 26 us; the launch traced here: 25.9 us
  Pallas kernels  24 us (92%)
  local copies, waits for them, and re-layouts  1.3 us (5%)
  between operations  0.64 us (2%)
    pallas_call x1, Pallas kernels, on_device(): pl.pallas_call(kernel, out_shape=(jax.ShapeDtypeStruct((PLANES * ROWS, CO...  24 us
    unnamed x2, local copies, waits for them, and re-layouts  1.3 us

profile of v5, /device:TPU:96, one launch (start us, length us, event | category | flops | bytes accessed | tf_op | source)
XLA Modules:
  0.0 25.9 jit_solution(6730108057972360977)
XLA Ops:
  0.6 24.0 %phase_linking.1 = (f32[512,128]{1,0:T(8,128)S(1)}, f32[8,128]{1,0:T(8,128)S(1)}) custom-call(s32[2,32]{1,0:T(2,128)} %offs_in.1, f32[2,8,4096]{2,1,0:T(8,128)} %bitcast.3, s32[5,8,128]{2,1,0:T(8,128)} %mask_in.1), custom_call_target="tpu_custom_call" | custom-call | tf_op jit(solution)/shard_map/phase_linking/pallas_call | solution.py:399
  24.6 0.7 %copy.7 = f32[2,32,8,128]{3,2,1,0:T(8,128)} copy(f32[2,32,8,128]{3,2,1,0:T(8,128)S(1)} %bitcast.2) | data formatting | bytes 524288
  25.3 0.6 %copy.8 = f32[8,128]{1,0:T(8,128)} copy(f32[8,128]{1,0:T(8,128)S(1)} %get-tuple-element.9) | data formatting | bytes 8192

commit v6 on v5

--- a/solution.py
+++ b/solution.py
@@ -43,6 +43,8 @@
 
 
 CHIPS = sorted(((g, i) for g in range(4) for i in range(4)), key=hops)
+FAR = CHIPS[11:]
+NEAR = CHIPS[:11]
 SENDS = [(g, i, k) for g, i in CHIPS for k in range(2) if (g, i, k) != (0, 0, 0)]
 
 
@@ -100,6 +102,7 @@
     rim_here,
     main_ref,
     rim_ref,
+    slab,
     mixed,
     tall,
     rim_tall,
@@ -113,6 +116,10 @@
     recv_sem,
     fwd_send,
     fwd_recv,
+    hop_send,
+    hop_recv,
+    far_send,
+    far_recv,
 ):
     date_pos, row_pos = lax.axis_index("date"), lax.axis_index("row")
     last_date, last_row = lax.axis_size("date") - 1, lax.axis_size("row") - 1
@@ -136,10 +143,82 @@
         )
 
     load.wait()
+    pl.semaphore_wait(barrier, NDATE + 1)
+
+    def part(which, date):
+        return (
+            (slc_here.at[:, :, pl.ds(pl.multiple_of(date * COLS, COLS), COLS)], main_ref)
+            if which == 0
+            else (rim_here.at[date], rim_ref)
+        )
+
+    def send(which, g, i, k):
+        dest = peer(date_pos, g, i, k)
+        src, ref = part(which, dest)
+        return pltpu.make_async_remote_copy(
+            src_ref=src,
+            dst_ref=ref.at[1, date_pos],
+            send_sem=send_sem.at[which, g, 2 * i + k],
+            recv_sem=recv_sem.at[which, g, 2 * i + k],
+            device_id={"date": dest},
+            device_id_type=MESH,
+        )
+
+    def sends_to(side):
+        return row_pos > 0 if side == 0 else row_pos < last_row
+
+    def gets_from(side):
+        return row_pos < last_row if side == 0 else row_pos > 0
+
+    def hop(side, n):
+        g, i = FAR[n]
+        chip = (date_pos // 8 + g) % 4 * 4 + (date_pos // 2 + i) % 4
+        cols = pl.ds(pl.multiple_of(chip * 2 * COLS, 2 * COLS), 2 * COLS)
+        return pltpu.make_async_remote_copy(
+            src_ref=slc_here.at[:, :, cols],
+            dst_ref=slab.at[side, :, :, cols],
+            send_sem=hop_send.at[side, n],
+            recv_sem=hop_recv.at[side, n],
+            device_id={"row": row_pos - 1 if side == 0 else row_pos + 1},
+            device_id_type=MESH,
+        )
+
+    def far(side, n, k):
+        dest = peer(date_pos, *FAR[n], k)
+        return pltpu.make_async_remote_copy(
+            src_ref=slab.at[side, :, :, pl.ds(pl.multiple_of(dest * COLS, COLS), COLS)],
+            dst_ref=main_ref.at[2 - 2 * side, date_pos],
+            send_sem=far_send.at[side, n, k],
+            recv_sem=far_recv.at[side, n, k],
+            device_id={"date": dest},
+            device_id_type=MESH,
+        )
+
+    hops_out = [[hop(side, n) for n in range(len(FAR))] for side in range(2)]
+    fars = [[far(side, n, k) for n in range(len(FAR)) for k in range(2)] for side in range(2)]
+    for side in range(2):
+
+        @pl.when(sends_to(side))
+        def _(side=side):
+            for copy in hops_out[side]:
+                copy.start()
+
+    mains = {step: send(0, *step) for step in SENDS}
+    rims = {step: send(1, *step) for step in SENDS}
+    for copy in mains.values():
+        copy.start()
     pack_rim(slc_here, rim_here)
+    own = []
+    for which in range(2):
+        src, ref = part(which, date_pos)
+        own.append(pltpu.make_async_copy(src, ref.at[1, date_pos], own_sem.at[which]))
+    for copy in own:
+        copy.start()
+    for copy in rims.values():
+        copy.start()
+
     load_mask.wait()
     load_offs.wait()
-
     population = jnp.zeros((8, COLS), jnp.int32)
     for w in range(5):
         population = population + lax.population_count(mask_ref[w])
@@ -156,39 +235,6 @@
                 pieces.append(zero8)
         slots[r] = jnp.concatenate(pieces, axis=0).T
 
-    pl.semaphore_wait(barrier, NDATE + 1)
-
-    def part(which, date):
-        return (
-            (slc_here.at[:, :, pl.ds(pl.multiple_of(date * COLS, COLS), COLS)], main_ref)
-            if which == 0
-            else (rim_here.at[date], rim_ref)
-        )
-
-    def send(which, g, i, k):
-        dest = peer(date_pos, g, i, k)
-        src, ref = part(which, dest)
-        return pltpu.make_async_remote_copy(
-            src_ref=src,
-            dst_ref=ref.at[1, date_pos],
-            send_sem=send_sem.at[which, g, 2 * i + k],
-            recv_sem=recv_sem.at[which, g, 2 * i + k],
-            device_id={"date": dest},
-            device_id_type=MESH,
-        )
-
-    mains = {step: send(0, *step) for step in SENDS}
-    rims = {step: send(1, *step) for step in SENDS}
-    for copy in mains.values():
-        copy.start()
-    own = []
-    for which in range(2):
-        src, ref = part(which, date_pos)
-        own.append(pltpu.make_async_copy(src, ref.at[1, date_pos], own_sem.at[which]))
-    for copy in own:
-        copy.start()
-    for copy in rims.values():
-        copy.start()
 
     def forward(side, number, first, count, ref):
         slot, to = (2, row_pos - 1) if side == 0 else (0, row_pos + 1)
@@ -203,15 +249,15 @@
 
     def forwards(side):
         out = []
-        for number, (g, i) in enumerate(CHIPS):
+        for number, (g, i) in enumerate(NEAR):
             first = (date_pos // 8 + 4 - g) % 4 * 8 + (date_pos // 2 + 4 - i) % 4 * 2
             out.append(forward(side, number, first, 2, main_ref))
-        return out + [forward(side, len(CHIPS), 0, NDATE, rim_ref)]
+        return out + [forward(side, len(NEAR), 0, NDATE, rim_ref)]
 
     before, after = forwards(0), forwards(1)
-    for number in range(len(CHIPS) + 1):
-        if number < len(CHIPS):
-            g, i = CHIPS[number]
+    for number in range(len(NEAR) + 1):
+        if number < len(NEAR):
+            g, i = NEAR[number]
             for k in range(2):
                 if (g, i, k) in mains:
                     mains[g, i, k].wait_recv()
@@ -230,19 +276,43 @@
         def _(number=number):
             after[number].start()
 
+        if number < len(FAR):
+            for side in range(2):
+
+                @pl.when(gets_from(side))
+                def _(side=side, number=number):
+                    hops_out[side][number].wait_recv()
+                    fars[side][2 * number].start()
+                    fars[side][2 * number + 1].start()
+
+    for g, i in FAR:
+        for k in range(2):
+            mains[g, i, k].wait_recv()
+    for side in range(2):
+
+        @pl.when(sends_to(side))
+        def _(side=side):
+            for copy in hops_out[side]:
+                copy.wait_send()
+
+        @pl.when(gets_from(side))
+        def _(side=side):
+            for copy in fars[side]:
+                copy.wait()
+
     for step in SENDS:
         mains[step].wait_send()
         rims[step].wait_send()
 
     @pl.when(row_pos > 0)
     def _():
-        for number in range(len(CHIPS) + 1):
+        for number in range(len(NEAR) + 1):
             before[number].wait_send()
             after[number].wait_recv()
 
     @pl.when(row_pos < last_row)
     def _():
-        for number in range(len(CHIPS) + 1):
+        for number in range(len(NEAR) + 1):
             after[number].wait_send()
             before[number].wait_recv()
 
@@ -411,6 +481,7 @@
             pltpu.VMEM((NDATE, 2, COLS), F32),
             pltpu.VMEM((3, NDATE, 2, ROWS, COLS), F32),
             pltpu.VMEM((3, NDATE, 2, COLS), F32),
+            pltpu.VMEM((2, 2, ROWS, NDATE * COLS), F32),
             pltpu.VMEM((WIN, PLANES, COLS), F32),
             pltpu.VMEM((8, 144, COLS), F32),
             pltpu.VMEM((3, COLS, COLS), F32),
@@ -422,8 +493,12 @@
             pltpu.SemaphoreType.DMA((5,)),
             pltpu.SemaphoreType.DMA((2, 4, 8)),
             pltpu.SemaphoreType.DMA((2, 4, 8)),
-            pltpu.SemaphoreType.DMA((2, 17)),
-            pltpu.SemaphoreType.DMA((2, 17)),
+            pltpu.SemaphoreType.DMA((2, len(NEAR) + 1)),
+            pltpu.SemaphoreType.DMA((2, len(NEAR) + 1)),
+            pltpu.SemaphoreType.DMA((2, len(FAR))),
+            pltpu.SemaphoreType.DMA((2, len(FAR))),
+            pltpu.SemaphoreType.DMA((2, len(FAR), 2)),
+            pltpu.SemaphoreType.DMA((2, len(FAR), 2)),
         ],
         compiler_params=pltpu.CompilerParams(
             collective_id=0, has_side_effects=True, vmem_limit_bytes=48 * 1024 * 1024

time: 26 us -> 25.4 us (0.977)
  Pallas kernels: 24 us -> 23.3 us
    pallas_call x1, Pallas kernels: 24 us -> 23.3 us  [on_device(): pl.pallas_call(kernel, out_shape=(jax.ShapeDtypeStruct((PLANES * ROWS, CO...]
where the time goes in v6:
time: 25.4 us; the launch traced here: 25.3 us
  Pallas kernels  23.3 us (92%)
  local copies, waits for them, and re-layouts  1.3 us (5%)
  between operations  0.64 us (3%)
    pallas_call x1, Pallas kernels, on_device(): pl.pallas_call(kernel, out_shape=(jax.ShapeDtypeStruct((PLANES * ROWS, CO...  23.3 us
    unnamed x2, local copies, waits for them, and re-layouts  1.3 us

profile of v6, /device:TPU:96, one launch (start us, length us, event | category | flops | bytes accessed | tf_op | source)
XLA Modules:
  0.0 25.3 jit_solution(2187897301947841457)
XLA Ops:
  0.6 23.3 %phase_linking.1 = (f32[512,128]{1,0:T(8,128)S(1)}, f32[8,128]{1,0:T(8,128)S(1)}) custom-call(s32[2,32]{1,0:T(2,128)} %offs_in.1, f32[2,8,4096]{2,1,0:T(8,128)} %bitcast.3, s32[5,8,128]{2,1,0:T(8,128)} %mask_in.1), custom_call_target="tpu_custom_call" | custom-call | tf_op jit(solution)/shard_map/phase_linking/pallas_call | solution.py:469
  24.0 0.7 %copy.7 = f32[2,32,8,128]{3,2,1,0:T(8,128)} copy(f32[2,32,8,128]{3,2,1,0:T(8,128)S(1)} %bitcast.2) | data formatting | bytes 524288
  24.7 0.6 %copy.8 = f32[8,128]{1,0:T(8,128)} copy(f32[8,128]{1,0:T(8,128)S(1)} %get-tuple-element.9) | data formatting | bytes 8192

commit v7 on v6

--- a/solution.py
+++ b/solution.py
@@ -43,8 +43,8 @@
 
 
 CHIPS = sorted(((g, i) for g in range(4) for i in range(4)), key=hops)
-FAR = CHIPS[11:]
-NEAR = CHIPS[:11]
+FAR = CHIPS[12:]
+NEAR = CHIPS[:12]
 SENDS = [(g, i, k) for g, i in CHIPS for k in range(2) if (g, i, k) != (0, 0, 0)]
 
 
@@ -290,31 +290,12 @@
             mains[g, i, k].wait_recv()
     for side in range(2):
 
-        @pl.when(sends_to(side))
-        def _(side=side):
-            for copy in hops_out[side]:
-                copy.wait_send()
-
         @pl.when(gets_from(side))
         def _(side=side):
             for copy in fars[side]:
-                copy.wait()
-
-    for step in SENDS:
-        mains[step].wait_send()
-        rims[step].wait_send()
-
-    @pl.when(row_pos > 0)
-    def _():
-        for number in range(len(NEAR) + 1):
-            before[number].wait_send()
-            after[number].wait_recv()
-
-    @pl.when(row_pos < last_row)
-    def _():
-        for number in range(len(NEAR) + 1):
-            after[number].wait_send()
-            before[number].wait_recv()
+                copy.wait_recv()
+            for copy in (before, after)[side][:-1]:
+                copy.wait_recv()
 
     main_rows = main_ref.reshape(-1, COLS)
     row_steps = date_vectors(offs_ref, 0)
@@ -334,6 +315,14 @@
             for i, x in enumerate(mix_rows(rows, row_steps[eight])):
                 mixed[i, part * NDATE + eight * 8 : part * NDATE + eight * 8 + 8, :] = x
 
+    for m in range(8):
+        tall[m, 8:136, :] = jnp.concatenate([mixed[2 * m], mixed[2 * m + 1]], axis=0).T
+    for side in range(2):
+
+        @pl.when(gets_from(side))
+        def _(side=side):
+            (before, after)[side][-1].wait_recv()
+
     for slot in range(3):
         x = jnp.concatenate([rim_ref[slot, :, 0, :], rim_ref[slot, :, 1, :]], axis=0)
         if slot == 0:
@@ -352,8 +341,6 @@
                 lane8 < PLANES, done[2 * m], done[2 * m + 1]
             )
 
-    for m in range(8):
-        tall[m, 8:136, :] = jnp.concatenate([mixed[2 * m], mixed[2 * m + 1]], axis=0).T
     for m in range(8):
         row = 8 * row_pos - 4 + 2 * m + (lane8 >= PLANES).astype(jnp.int32)
         inside = (row >= 0) & (row < 8 * (last_row + 1))
@@ -461,6 +448,32 @@
         root1 = jnp.sqrt(n1 + EPSILON)
         eigen_ref[r : r + 1, :] = root2 / root1
         out_ref[pl.ds(r, PLANES, stride=ROWS), :] = x2 * (jnp.sqrt(F32(NDATE)) / root2)
+
+    for step in SENDS:
+        mains[step].wait_send()
+        rims[step].wait_send()
+    for side in range(2):
+
+        @pl.when(sends_to(side))
+        def _(side=side):
+            for copy in hops_out[side] + (before, after)[side]:
+                copy.wait_send()
+
+        @pl.when(gets_from(side))
+        def _(side=side):
+            for copy in fars[side]:
+                copy.wait_send()
+
+
+def hand_out(linked_ref, eigen_ref, linked_out, eigen_out, sem):
+    copies = [
+        pltpu.make_async_copy(linked_ref, linked_out, sem.at[0]),
+        pltpu.make_async_copy(eigen_ref, eigen_out, sem.at[1]),
+    ]
+    for copy in copies:
+        copy.start()
+    for copy in copies:
+        copy.wait()
 
 
 def on_device(slc, offsets, masks):
@@ -505,6 +518,17 @@
         ),
         name="phase_linking",
     )(*(pltpu.with_memory_space_constraint(x, pltpu.HBM) for x in (offsets, slc[:, 0], masks)))
+    linked, eigen = pl.pallas_call(
+        hand_out,
+        out_shape=(
+            jax.ShapeDtypeStruct((PLANES * ROWS, COLS), F32),
+            jax.ShapeDtypeStruct((ROWS, COLS), F32),
+        ),
+        in_specs=[vmem, vmem],
+        out_specs=(hbm, hbm),
+        scratch_shapes=[pltpu.SemaphoreType.DMA((2,))],
+        name="hand_out",
+    )(*(pltpu.with_memory_space_constraint(x, pltpu.VMEM) for x in (linked, eigen)))
     return linked.reshape(2, NDATE, ROWS, COLS), eigen
 
 

time: 25.4 us -> 24.5 us (0.965)
  local copies, waits for them, and re-layouts: 1.3 us -> 0 us
  Pallas kernels: 23.3 us -> 23.7 us
    unnamed x2 -> x0, local copies, waits for them, and re-layouts: 1.3 us -> none
    pallas_call x0 -> x1, Pallas kernels: none -> 0.72 us  [on_device(): pl.pallas_call(hand_out, out_shape=(jax.ShapeDtypeStruct((PLANES * ROWS,...]
    pallas_call x1, Pallas kernels: 23.3 us -> 22.9 us  [on_device(): pl.pallas_call(kernel, out_shape=(jax.ShapeDtypeStruct((PLANES * ROWS, CO...]
where the time goes in v7:
time: 24.5 us; the launch traced here: 24.3 us
  Pallas kernels  23.7 us (97%)
  between operations  0.64 us (3%)
    pallas_call x1, Pallas kernels, on_device(): pl.pallas_call(kernel, out_shape=(jax.ShapeDtypeStruct((PLANES * ROWS, CO...  22.9 us
    pallas_call x1, Pallas kernels, on_device(): pl.pallas_call(hand_out, out_shape=(jax.ShapeDtypeStruct((PLANES * ROWS,...  0.72 us

profile of v7, /device:TPU:96, one launch (start us, length us, event | category | flops | bytes accessed | tf_op | source)
XLA Modules:
  0.0 24.3 jit_solution(6154669146123665318)
XLA Ops:
  0.6 22.9 %phase_linking.1 = (f32[512,128]{1,0:T(8,128)S(1)}, f32[8,128]{1,0:T(8,128)S(1)}) custom-call(s32[2,32]{1,0:T(2,128)} %offs_in.1, f32[2,8,4096]{2,1,0:T(8,128)} %bitcast.2, s32[5,8,128]{2,1,0:T(8,128)} %mask_in.1), custom_call_target="tpu_custom_call" | custom-call | tf_op jit(solution)/shard_map/phase_linking/pallas_call | solution.py:482
  23.6 0.7 %hand_out.1 = (f32[512,128]{1,0:T(8,128)}, f32[8,128]{1,0:T(8,128)}) custom-call(f32[512,128]{1,0:T(8,128)S(1)} %get-tuple-element.6.linked_ref, f32[8,128]{1,0:T(8,128)S(1)} %get-tuple-element.7.eigen_ref), custom_call_target="tpu_custom_call" | custom-call | tf_op jit(solution)/shard_map/hand_out/pallas_call | solution.py:521

commit v8 on v7

--- a/solution.py
+++ b/solution.py
@@ -88,6 +88,10 @@
     return [
         0.5625 * (base[i + 1] + base[i + 2]) - 0.0625 * (base[i] + base[i + 3]) for i in range(WIN)
     ]
+
+
+def all_of(ref, sem):
+    pltpu.make_async_copy(ref, ref, sem).wait()
 
 
 def kernel(
@@ -158,8 +162,12 @@
         return pltpu.make_async_remote_copy(
             src_ref=src,
             dst_ref=ref.at[1, date_pos],
-            send_sem=send_sem.at[which, g, 2 * i + k],
-            recv_sem=recv_sem.at[which, g, 2 * i + k],
+            send_sem=send_sem.at[which],
+            recv_sem=own_sem.at[1]
+            if which
+            else own_sem.at[5]
+            if (g, i) in FAR
+            else recv_sem.at[g, 2 * i + k],
             device_id={"date": dest},
             device_id_type=MESH,
         )
@@ -177,7 +185,7 @@
         return pltpu.make_async_remote_copy(
             src_ref=slc_here.at[:, :, cols],
             dst_ref=slab.at[side, :, :, cols],
-            send_sem=hop_send.at[side, n],
+            send_sem=hop_send.at[side],
             recv_sem=hop_recv.at[side, n],
             device_id={"row": row_pos - 1 if side == 0 else row_pos + 1},
             device_id_type=MESH,
@@ -188,8 +196,8 @@
         return pltpu.make_async_remote_copy(
             src_ref=slab.at[side, :, :, pl.ds(pl.multiple_of(dest * COLS, COLS), COLS)],
             dst_ref=main_ref.at[2 - 2 * side, date_pos],
-            send_sem=far_send.at[side, n, k],
-            recv_sem=far_recv.at[side, n, k],
+            send_sem=far_send.at[side],
+            recv_sem=far_recv.at[side],
             device_id={"date": dest},
             device_id_type=MESH,
         )
@@ -241,8 +249,8 @@
         return pltpu.make_async_remote_copy(
             src_ref=ref.at[1, pl.ds(first, count)],
             dst_ref=ref.at[slot, pl.ds(first, count)],
-            send_sem=fwd_send.at[side, number],
-            recv_sem=fwd_recv.at[side, number],
+            send_sem=fwd_send.at[side, number // len(NEAR)],
+            recv_sem=fwd_recv.at[side, number // len(NEAR)],
             device_id={"row": to},
             device_id_type=MESH,
         )
@@ -264,9 +272,7 @@
                 else:
                     own[0].wait()
         else:
-            own[1].wait()
-            for copy in rims.values():
-                copy.wait_recv()
+            all_of(rim_ref.at[1], own_sem.at[1])
 
         @pl.when(row_pos > 0)
         def _(number=number):
@@ -285,17 +291,16 @@
                     fars[side][2 * number].start()
                     fars[side][2 * number + 1].start()
 
-    for g, i in FAR:
-        for k in range(2):
-            mains[g, i, k].wait_recv()
+    all_of(main_ref.at[1, pl.ds(0, NDATE - 1)], send_sem.at[0])
+    all_of(rim_ref.at[1, pl.ds(0, NDATE - 1)], send_sem.at[1])
+    all_of(main_ref.at[1, pl.ds(0, 2 * len(FAR))], own_sem.at[5])
     for side in range(2):
 
         @pl.when(gets_from(side))
         def _(side=side):
-            for copy in fars[side]:
-                copy.wait_recv()
-            for copy in (before, after)[side][:-1]:
-                copy.wait_recv()
+            all_of(main_ref.at[1, pl.ds(0, 2 * len(FAR))], far_send.at[side])
+            all_of(main_ref.at[1, pl.ds(0, 2 * len(FAR))], far_recv.at[side])
+            all_of(main_ref.at[1, pl.ds(0, 2 * len(NEAR))], fwd_recv.at[side, 0])
 
     main_rows = main_ref.reshape(-1, COLS)
     row_steps = date_vectors(offs_ref, 0)
@@ -321,7 +326,7 @@
 
         @pl.when(gets_from(side))
         def _(side=side):
-            (before, after)[side][-1].wait_recv()
+            all_of(rim_ref.at[1], fwd_recv.at[side, 1])
 
     for slot in range(3):
         x = jnp.concatenate([rim_ref[slot, :, 0, :], rim_ref[slot, :, 1, :]], axis=0)
@@ -449,20 +454,13 @@
         eigen_ref[r : r + 1, :] = root2 / root1
         out_ref[pl.ds(r, PLANES, stride=ROWS), :] = x2 * (jnp.sqrt(F32(NDATE)) / root2)
 
-    for step in SENDS:
-        mains[step].wait_send()
-        rims[step].wait_send()
     for side in range(2):
 
         @pl.when(sends_to(side))
         def _(side=side):
-            for copy in hops_out[side] + (before, after)[side]:
-                copy.wait_send()
-
-        @pl.when(gets_from(side))
-        def _(side=side):
-            for copy in fars[side]:
-                copy.wait_send()
+            all_of(main_ref.at[1, pl.ds(0, 2 * len(FAR))], hop_send.at[side])
+            all_of(main_ref.at[1, pl.ds(0, 2 * len(NEAR))], fwd_send.at[side, 0])
+            all_of(rim_ref.at[1], fwd_send.at[side, 1])
 
 
 def hand_out(linked_ref, eigen_ref, linked_out, eigen_out, sem):
@@ -503,15 +501,15 @@
             pltpu.VMEM((GROUPS * COLS, 2 * COLS), BF16),
             pltpu.VMEM((8, COLS, COLS), jnp.int32),
             pltpu.VMEM((8, COLS, COLS), F32),
-            pltpu.SemaphoreType.DMA((5,)),
-            pltpu.SemaphoreType.DMA((2, 4, 8)),
-            pltpu.SemaphoreType.DMA((2, 4, 8)),
-            pltpu.SemaphoreType.DMA((2, len(NEAR) + 1)),
-            pltpu.SemaphoreType.DMA((2, len(NEAR) + 1)),
+            pltpu.SemaphoreType.DMA((6,)),
+            pltpu.SemaphoreType.DMA((2,)),
+            pltpu.SemaphoreType.DMA((4, 8)),
+            pltpu.SemaphoreType.DMA((2, 2)),
+            pltpu.SemaphoreType.DMA((2, 2)),
+            pltpu.SemaphoreType.DMA((2,)),
             pltpu.SemaphoreType.DMA((2, len(FAR))),
-            pltpu.SemaphoreType.DMA((2, len(FAR))),
-            pltpu.SemaphoreType.DMA((2, len(FAR), 2)),
-            pltpu.SemaphoreType.DMA((2, len(FAR), 2)),
+            pltpu.SemaphoreType.DMA((2,)),
+            pltpu.SemaphoreType.DMA((2,)),
         ],
         compiler_params=pltpu.CompilerParams(
             collective_id=0, has_side_effects=True, vmem_limit_bytes=48 * 1024 * 1024

time: 24.5 us -> 22.8 us (0.931)
  Pallas kernels: 23.7 us -> 22 us
    pallas_call x1, Pallas kernels: 22.9 us -> 21.2 us  [on_device(): pl.pallas_call(kernel, out_shape=(jax.ShapeDtypeStruct((PLANES * ROWS, CO...]
where the time goes in v8:
time: 22.8 us; the launch traced here: 22.6 us
  Pallas kernels  22 us (96%)
  between operations  0.64 us (3%)
    pallas_call x1, Pallas kernels, on_device(): pl.pallas_call(kernel, out_shape=(jax.ShapeDtypeStruct((PLANES * ROWS, CO...  21.2 us
    pallas_call x1, Pallas kernels, on_device(): pl.pallas_call(hand_out, out_shape=(jax.ShapeDtypeStruct((PLANES * ROWS,...  0.72 us

profile of v8, /device:TPU:96, one launch (start us, length us, event | category | flops | bytes accessed | tf_op | source)
XLA Modules:
  0.0 22.6 jit_solution(10670710673698497622)
XLA Ops:
  0.6 21.2 %phase_linking.1 = (f32[512,128]{1,0:T(8,128)S(1)}, f32[8,128]{1,0:T(8,128)S(1)}) custom-call(s32[2,32]{1,0:T(2,128)} %offs_in.1, f32[2,8,4096]{2,1,0:T(8,128)} %bitcast.2, s32[5,8,128]{2,1,0:T(8,128)} %mask_in.1), custom_call_target="tpu_custom_call" | custom-call | tf_op jit(solution)/shard_map/phase_linking/pallas_call | solution.py:480
  21.9 0.7 %hand_out.1 = (f32[512,128]{1,0:T(8,128)}, f32[8,128]{1,0:T(8,128)}) custom-call(f32[512,128]{1,0:T(8,128)S(1)} %get-tuple-element.6.linked_ref, f32[8,128]{1,0:T(8,128)S(1)} %get-tuple-element.7.eigen_ref), custom_call_target="tpu_custom_call" | custom-call | tf_op jit(solution)/shard_map/hand_out/pallas_call | solution.py:519

commit v9 on v8

--- a/solution.py
+++ b/solution.py
@@ -147,6 +147,7 @@
         )
 
     load.wait()
+    pack_rim(slc_here, rim_here)
     pl.semaphore_wait(barrier, NDATE + 1)
 
     def part(which, date):
@@ -167,7 +168,7 @@
             if which
             else own_sem.at[5]
             if (g, i) in FAR
-            else recv_sem.at[g, 2 * i + k],
+            else recv_sem.at[g, i],
             device_id={"date": dest},
             device_id_type=MESH,
         )
@@ -213,16 +214,18 @@
 
     mains = {step: send(0, *step) for step in SENDS}
     rims = {step: send(1, *step) for step in SENDS}
-    for copy in mains.values():
-        copy.start()
-    pack_rim(slc_here, rim_here)
+    for step in SENDS:
+        mains[step].start()
+        rims[step].start()
     own = []
     for which in range(2):
         src, ref = part(which, date_pos)
-        own.append(pltpu.make_async_copy(src, ref.at[1, date_pos], own_sem.at[which]))
+        own.append(
+            pltpu.make_async_copy(
+                src, ref.at[1, date_pos], own_sem.at[1] if which else recv_sem.at[0, 0]
+            )
+        )
     for copy in own:
-        copy.start()
-    for copy in rims.values():
         copy.start()
 
     load_mask.wait()
@@ -266,30 +269,25 @@
     for number in range(len(NEAR) + 1):
         if number < len(NEAR):
             g, i = NEAR[number]
-            for k in range(2):
-                if (g, i, k) in mains:
-                    mains[g, i, k].wait_recv()
-                else:
-                    own[0].wait()
+            all_of(main_ref.at[1, pl.ds(0, 2)], recv_sem.at[g, i])
         else:
             all_of(rim_ref.at[1], own_sem.at[1])
 
         @pl.when(row_pos > 0)
         def _(number=number):
             before[number].start()
+            if number < len(FAR):
+                hops_out[1][number].wait_recv()
+                fars[1][2 * number].start()
+                fars[1][2 * number + 1].start()
 
         @pl.when(row_pos < last_row)
         def _(number=number):
             after[number].start()
-
-        if number < len(FAR):
-            for side in range(2):
-
-                @pl.when(gets_from(side))
-                def _(side=side, number=number):
-                    hops_out[side][number].wait_recv()
-                    fars[side][2 * number].start()
-                    fars[side][2 * number + 1].start()
+            if number < len(FAR):
+                hops_out[0][number].wait_recv()
+                fars[0][2 * number].start()
+                fars[0][2 * number + 1].start()
 
     all_of(main_ref.at[1, pl.ds(0, NDATE - 1)], send_sem.at[0])
     all_of(rim_ref.at[1, pl.ds(0, NDATE - 1)], send_sem.at[1])
@@ -503,7 +501,7 @@
             pltpu.VMEM((8, COLS, COLS), F32),
             pltpu.SemaphoreType.DMA((6,)),
             pltpu.SemaphoreType.DMA((2,)),
-            pltpu.SemaphoreType.DMA((4, 8)),
+            pltpu.SemaphoreType.DMA((4, 4)),
             pltpu.SemaphoreType.DMA((2, 2)),
             pltpu.SemaphoreType.DMA((2, 2)),
             pltpu.SemaphoreType.DMA((2,)),

time: 22.8 us -> 22.7 us (level)
  Pallas kernels: 22 us -> 21.7 us
    pallas_call x1, Pallas kernels: 21.2 us -> 21 us  [on_device(): pl.pallas_call(kernel, out_shape=(jax.ShapeDtypeStruct((PLANES * ROWS, CO...]
where the time goes in v9:
time: 22.7 us; the launch traced here: 22.3 us
  Pallas kernels  21.7 us (96%)
  between operations  0.64 us (3%)
    pallas_call x1, Pallas kernels, on_device(): pl.pallas_call(kernel, out_shape=(jax.ShapeDtypeStruct((PLANES * ROWS, CO...  21 us
    pallas_call x1, Pallas kernels, on_device(): pl.pallas_call(hand_out, out_shape=(jax.ShapeDtypeStruct((PLANES * ROWS,...  0.72 us

profile of v9, /device:TPU:96, one launch (start us, length us, event | category | flops | bytes accessed | tf_op | source)
XLA Modules:
  0.0 22.3 jit_solution(7679137996741806631)
XLA Ops:
  0.6 21.0 %phase_linking.1 = (f32[512,128]{1,0:T(8,128)S(1)}, f32[8,128]{1,0:T(8,128)S(1)}) custom-call(s32[2,32]{1,0:T(2,128)} %offs_in.1, f32[2,8,4096]{2,1,0:T(8,128)} %bitcast.2, s32[5,8,128]{2,1,0:T(8,128)} %mask_in.1), custom_call_target="tpu_custom_call" | custom-call | tf_op jit(solution)/shard_map/phase_linking/pallas_call | solution.py:478
  21.6 0.7 %hand_out.1 = (f32[512,128]{1,0:T(8,128)}, f32[8,128]{1,0:T(8,128)}) custom-call(f32[512,128]{1,0:T(8,128)S(1)} %get-tuple-element.6.linked_ref, f32[8,128]{1,0:T(8,128)S(1)} %get-tuple-element.7.eigen_ref), custom_call_target="tpu_custom_call" | custom-call | tf_op jit(solution)/shard_map/hand_out/pallas_call | solution.py:517

commit v10 on v9

--- a/solution.py
+++ b/solution.py
@@ -39,7 +39,8 @@
 
 
 def hops(step):
-    return min(step[0], 4 - step[0]) + min(step[1], 4 - step[1])
+    along_y, along_x = (min(n, 4 - n) for n in step)
+    return along_y + along_x, along_y
 
 
 CHIPS = sorted(((g, i) for g in range(4) for i in range(4)), key=hops)

time: 22.7 us -> 22.5 us (level)
  no operation moved by 1% of the time
where the time goes in v10:
time: 22.5 us; the launch traced here: 22.2 us
  Pallas kernels  21.6 us (96%)
  between operations  0.64 us (3%)
    pallas_call x1, Pallas kernels, on_device(): pl.pallas_call(kernel, out_shape=(jax.ShapeDtypeStruct((PLANES * ROWS, CO...  20.8 us
    pallas_call x1, Pallas kernels, on_device(): pl.pallas_call(hand_out, out_shape=(jax.ShapeDtypeStruct((PLANES * ROWS,...  0.72 us

profile of v10, /device:TPU:96, one launch (start us, length us, event | category | flops | bytes accessed | tf_op | source)
XLA Modules:
  0.0 22.2 jit_solution(16448764849399882633)
XLA Ops:
  0.6 20.8 %phase_linking.1 = (f32[512,128]{1,0:T(8,128)S(1)}, f32[8,128]{1,0:T(8,128)S(1)}) custom-call(s32[2,32]{1,0:T(2,128)} %offs_in.1, f32[2,8,4096]{2,1,0:T(8,128)} %bitcast.2, s32[5,8,128]{2,1,0:T(8,128)} %mask_in.1), custom_call_target="tpu_custom_call" | custom-call | tf_op jit(solution)/shard_map/phase_linking/pallas_call | solution.py:479
  21.5 0.7 %hand_out.1 = (f32[512,128]{1,0:T(8,128)}, f32[8,128]{1,0:T(8,128)}) custom-call(f32[512,128]{1,0:T(8,128)S(1)} %get-tuple-element.6.linked_ref, f32[8,128]{1,0:T(8,128)S(1)} %get-tuple-element.7.eigen_ref), custom_call_target="tpu_custom_call" | custom-call | tf_op jit(solution)/shard_map/hand_out/pallas_call | solution.py:518
